TPU v7x, 256 devices: a whole 4x4x8 slice. The times are simulated.
256 devices in a mesh: down: 32 (over z_hi, y, core), cross: 8 (over z_lo, x).
Axes of the slice: x: 4, y: 4, z: 8 (z_hi: 4, z_lo: 2; z = z_hi * 2 + z_lo), core: 2. Of those that a mesh axis runs over, the one named last changes fastest.
Arguments:
- particles: float32 [32768, 12, 128], P(('down', 'cross')), may hold values from -4 to 14.5, as said below
- anchor_down: int32 [2, 32768], P(None, ('down', 'cross')), may hold values from -4 to 12
- anchor_cross: int32 [2, 32768], P(None, ('down', 'cross')), may hold values from -4 to 244
- move_count: int32 [2, 4, 32, 8], P(None, None, 'down', 'cross'), may hold values from 0 to 13, as said below
- move_slots: int32 [2, 4, 13, 32, 8], P(None, None, None, 'down', 'cross'), may hold values from 0 to 127, as said below
Outputs:
- moved_particles: float32 [32768, 12, 128], P(('down', 'cross'))
Inputs may be any that keep to these rules, and one draw needn't show every extreme that they name: `move_count`: entry 0 of tile (i, j) equals entry 1 of tile (i + 1, j), and entry 2 of (i, j) equals entry 3 of (i, j + 1); entries toward the outside of the grid are 0; in every step some link carries 13. `move_slots`: for each step and tile the 52 slot numbers are different. `particles`: field 0 lies in [0.5, 8 - 1.5] and field 1 in [0.5, 16 - 1.5]; fields 7 to 10 are positive.
All inputs are finite; a program needn't handle non-finite values.
Results may differ from a plain program's by a relative error of at most 0.0003.
Values sent between devices are 32-bit elements; how exact they have to be, the bound alone decides.
A program may use at most 64 MiB of HBM per device.

v0:
```python
import math

import jax
import jax.numpy as jnp
from jax import lax
from jax.sharding import PartitionSpec as P

WIN_DOWN = 8
WIN_CROSS = 16
GHOST = 4
STEPS = 2
MOVE_CAP = 13
TILE_DOWN = 16
TILE_CROSS = 256


TIME_STEP = 0.1
GRAVITY = 5.6
MASS_FLOOR = 0.5
HIGHEST = lax.Precision.HIGHEST
group_limit = 8


def padded(x, sides, width):
    for axis, dim in sides:
        size, length = (lax.axis_size(axis), x.shape[dim])
        up = [(i, (i + 1) % size) for i in range(size - 1)]
        down = [(j, i) for i, j in up]
        last = lax.slice_in_dim(x, length - width, length, axis=dim)
        initial = lax.slice_in_dim(x, 0, width, axis=dim)
        before = lax.ppermute(last, axis, up)
        after = lax.ppermute(initial, axis, down)
        x = jnp.concatenate([before, x, after], axis=dim)
    return x


def spline_pair(distance):
    magnitude = jnp.abs(distance)
    inside = 0.75 - distance * distance
    remote = 0.5 * (1.5 - magnitude) * (1.5 - magnitude)
    spline_value = jnp.where(magnitude < 0.5, inside, jnp.where(magnitude < 1.5, remote, 0.0))
    slope_far = jnp.where(distance > 0.0, distance - 1.5, distance + 1.5)
    spline_slope = jnp.where(
        magnitude < 0.5, -2.0 * distance, jnp.where(magnitude < 1.5, slope_far, 0.0)
    )
    return (spline_value, spline_slope)


def block_weights(block_group):
    node_index = jnp.arange(WIN_DOWN * WIN_CROSS)
    node_row = (node_index // WIN_CROSS).astype(block_group.dtype)
    node_col = (node_index % WIN_CROSS).astype(block_group.dtype)
    down_value, down_slope = spline_pair(block_group[:, 0, :, None] - node_row)
    cross_value, cross_slope = spline_pair(block_group[:, 1, :, None] - node_col)
    return (down_value * cross_value, down_slope * cross_value, down_value * cross_slope)


def scatter_terms(block_group):
    weight, grad_down, grad_cross = block_weights(block_group)
    mass_value = block_group[:, 7]
    volume_value = block_group[:, 8]
    carried = jnp.stack(
        [mass_value, mass_value * block_group[:, 2], mass_value * block_group[:, 3]], axis=1
    )
    stress_down = jnp.stack(
        [-volume_value * block_group[:, 4], -volume_value * block_group[:, 5]], axis=1
    )
    stress_cross = jnp.stack(
        [-volume_value * block_group[:, 5], -volume_value * block_group[:, 6]], axis=1
    )
    lumped = jnp.einsum("bcp,bpn->bcn", carried, weight, precision=HIGHEST)
    force_sum = jnp.einsum("bcp,bpn->bcn", stress_down, grad_down, precision=HIGHEST)
    force_sum = force_sum + jnp.einsum("bcp,bpn->bcn", stress_cross, grad_cross, precision=HIGHEST)
    return jnp.concatenate([lumped, force_sum], axis=1)


def advance(block_group, particle_vel, along_down, along_cross):
    rate_dd = along_down[:, 0]
    rate_cc = along_cross[:, 1]
    rate_dc = 0.5 * (along_cross[:, 0] + along_down[:, 1])
    trace_rate = rate_dd + rate_cc
    shear_value = block_group[:, 9]
    lame_value = block_group[:, 10]
    stress_dd = block_group[:, 4] + TIME_STEP * (
        lame_value * trace_rate + 2.0 * shear_value * rate_dd
    )
    stress_dc = block_group[:, 5] + TIME_STEP * (2.0 * shear_value * rate_dc)
    stress_cc = block_group[:, 6] + TIME_STEP * (
        lame_value * trace_rate + 2.0 * shear_value * rate_cc
    )
    offset_down = jnp.clip(block_group[:, 0] + TIME_STEP * particle_vel[:, 0], 0.5, WIN_DOWN - 1.5)
    offset_cross = jnp.clip(
        block_group[:, 1] + TIME_STEP * particle_vel[:, 1], 0.5, WIN_CROSS - 1.5
    )
    volume_value = block_group[:, 8] * (1.0 + TIME_STEP * trace_rate)
    strain_value = block_group[:, 11] + TIME_STEP * (
        rate_dd * rate_dd + rate_cc * rate_cc + 2.0 * rate_dc * rate_dc
    )
    return jnp.stack(
        [
            offset_down,
            offset_cross,
            particle_vel[:, 0],
            particle_vel[:, 1],
            stress_dd,
            stress_dc,
            stress_cc,
            block_group[:, 7],
            volume_value,
            shear_value,
            lame_value,
            strain_value,
        ],
        axis=1,
    )


def gather_terms(block_group, window_vel):
    weight, grad_down, grad_cross = block_weights(block_group)
    particle_vel = jnp.einsum("bcn,bpn->bcp", window_vel, weight, precision=HIGHEST)
    along_down = jnp.einsum("bcn,bpn->bcp", window_vel, grad_down, precision=HIGHEST)
    along_cross = jnp.einsum("bcn,bpn->bcp", window_vel, grad_cross, precision=HIGHEST)
    return advance(block_group, particle_vel, along_down, along_cross)


def by_groups(block_task, particle_state, *extra_args):
    block_count = particle_state.shape[0]
    group_size = math.gcd(block_count, group_limit)
    packed = tuple(
        (
            member.reshape((block_count // group_size, group_size) + member.shape[1:])
            for member in (particle_state,) + extra_args
        )
    )

    def run_group(pieces):
        return block_task(*pieces)

    result = lax.map(run_group, packed)
    return result.reshape((block_count,) + result.shape[2:])


def node_velocity(node_sums, keep_mask):
    mass_sum = node_sums[0]
    moved_sum = jnp.stack(
        [
            node_sums[1] + TIME_STEP * (node_sums[3] + GRAVITY * mass_sum),
            node_sums[2] + TIME_STEP * node_sums[4],
        ]
    )
    return jnp.where(keep_mask, moved_sum / jnp.maximum(mass_sum, MASS_FLOOR), 0.0)


def inside_mask(row_global, col_global, total_rows, total_cols):
    keep_rows = (row_global > 0) & (row_global < total_rows - 1)
    keep_cols = (col_global > 0) & (col_global < total_cols - 1)
    return keep_rows[:, None] & keep_cols[None, :]


def settle(particle_state, slot_list, count_value, incoming):
    valid_mask = (jnp.arange(MOVE_CAP, dtype=jnp.int32) < count_value)[:, None, None]
    return particle_state.at[slot_list].set(
        jnp.where(valid_mask, incoming, particle_state[slot_list])
    )


def on_device(particles, anchor_down, anchor_cross, move_count, move_slots):
    particle_state = particles
    grid_width = TILE_CROSS + 2 * GHOST
    grid_height = TILE_DOWN + 2 * GHOST
    node_index = jnp.arange(WIN_DOWN * WIN_CROSS, dtype=jnp.int32)
    node_row = node_index // WIN_CROSS
    node_col = node_index % WIN_CROSS
    row_start = lax.axis_index("down") * TILE_DOWN
    col_start = lax.axis_index("cross") * TILE_CROSS
    total_rows = TILE_DOWN * lax.axis_size("down")
    total_cols = TILE_CROSS * lax.axis_size("cross")
    inner_rows = row_start + jnp.arange(TILE_DOWN, dtype=jnp.int32)
    inner_cols = col_start + jnp.arange(TILE_CROSS, dtype=jnp.int32)
    for step_index in range(STEPS):
        first_row = anchor_down[step_index][:, None] + GHOST + node_row[None, :]
        first_col = anchor_cross[step_index][:, None] + GHOST + node_col[None, :]
        flat_index = first_row * grid_width + first_col
        node_terms = by_groups(scatter_terms, particle_state)
        spread = jnp.transpose(node_terms, (1, 0, 2)).reshape(5, -1)
        node_sums = (
            jnp.zeros((5, grid_height * grid_width), jnp.float32)
            .at[:, flat_index.reshape(-1)]
            .add(spread)
        )
        node_sums = node_sums.reshape(5, grid_height, grid_width)
        rim_band = jnp.concatenate(
            [node_sums[:, :GHOST], node_sums[:, TILE_DOWN + GHOST :]], axis=1
        )
        rim_sums = padded(rim_band, (("down", 1),), GHOST)
        core_sums = node_sums[:, GHOST : GHOST + TILE_DOWN]
        core_sums = core_sums.at[:, :GHOST].add(rim_sums[:, :GHOST])
        core_sums = core_sums.at[:, TILE_DOWN - GHOST :].add(rim_sums[:, 3 * GHOST :])
        rim_band = jnp.concatenate(
            [core_sums[:, :, :GHOST], core_sums[:, :, TILE_CROSS + GHOST :]], axis=2
        )
        rim_sums = padded(rim_band, (("cross", 2),), GHOST)
        core_sums = core_sums[:, :, GHOST : GHOST + TILE_CROSS]
        core_sums = core_sums.at[:, :, :GHOST].add(rim_sums[:, :, :GHOST])
        core_sums = core_sums.at[:, :, TILE_CROSS - GHOST :].add(rim_sums[:, :, 3 * GHOST :])
        core_velocity = node_velocity(
            core_sums, inside_mask(inner_rows, inner_cols, total_rows, total_cols)
        )
        window_grid = padded(core_velocity, (("down", 1), ("cross", 2)), GHOST)
        window_vel = jnp.transpose(window_grid.reshape(2, -1)[:, flat_index], (1, 0, 2))
        particle_state = by_groups(gather_terms, particle_state, window_vel)
        slot_list = move_slots[step_index][:, :, 0, 0]
        count_list = move_count[step_index][:, 0, 0]
        outgoing = jnp.concatenate(
            [particle_state[slot_list[1]], particle_state[slot_list[0]]], axis=0
        )
        arrived = padded(outgoing, (("down", 0),), MOVE_CAP)
        particle_state = settle(particle_state, slot_list[1], count_list[1], arrived[:MOVE_CAP])
        particle_state = settle(
            particle_state, slot_list[0], count_list[0], arrived[3 * MOVE_CAP :]
        )
        outgoing = jnp.concatenate(
            [particle_state[slot_list[3]], particle_state[slot_list[2]]], axis=0
        )
        arrived = padded(outgoing, (("cross", 0),), MOVE_CAP)
        particle_state = settle(particle_state, slot_list[3], count_list[3], arrived[:MOVE_CAP])
        particle_state = settle(
            particle_state, slot_list[2], count_list[2], arrived[3 * MOVE_CAP :]
        )
    return particle_state


def solution(mesh):
    return jax.shard_map(
        on_device,
        mesh=mesh,
        in_specs=(
            P(("down", "cross"), None, None),
            P(None, ("down", "cross")),
            P(None, ("down", "cross")),
            P(None, None, "down", "cross"),
            P(None, None, None, "down", "cross"),
        ),
        out_specs=P(("down", "cross"), None, None),
        check_vma=False,
    )
```

profile of v0, /device:TPU:95, one launch (start us, length us, event | category | flops | bytes accessed | tf_op | source)
XLA Modules:
  0.0 753.1 jit_solution(6102479055518349198)
XLA Ops:
  1.0 61.5 %while.60 = (s32[]{:T(128)}, f32[16,8,5,128]{3,2,1,0:T(8,128)S(1)}, f32[16,8,12,128]{3,1,0,2:T(8,128)}, s32[]{:T(128)}) while((s32[]{:T(128)}, f32[16,8,5,128]{3,2,1,0:T(8,128)S(1)}, f32[16,8,12,128]{3,1,0,2:T(8,128)}, s32[]{:T(128)}) %tuple.241), condition=%wide.region_1.2_spmd, body=%wide.region_0.1_spmd.sunk | while | flops 20079360 | bytes 417853 | solution.py:139
  62.6 4.9 copy.110
  67.4 88.4 %scatter_custom_fusion = f32[5,6336]{0,1:T(8,128)S(1)} fusion(s32[16384]{0:T(1024)S(1)} %bitcast.269, f32[16384,5]{1,0:T(8,128)} %bitcast.220, f32[]{:T(128)} %constant.678.clone.1), kind=kCustom, calls=%fused_computation.511 | custom fusion | flops 81920 | bytes 127232 | tf_op jit(solution)/shard_map/scatter-add | solution.py:189
  159.0 6.3 collective-permute-start
  166.6 1.9 collective-permute-start.1
  175.3 2.5 copy.148
  179.5 2.6 collective-permute-start.2
  182.2 2.7 collective-permute-start.3
  185.3 3.8 collective-permute-done.3
  190.1 9.2 %collective-permute-start.4 = (f32[2,4,256]{2,1,0:T(4,128)S(1)}, f32[2,4,256]{2,1,0:T(4,128)S(1)}, u32[]{:S(2)}, u32[]{:S(2)}) collective-permute-start(f32[2,4,256]{2,1,0:T(4,128)S(1)} %get-tuple-element.519), channel_id=1, source_target_pairs={{0,8},{8,16},{16,24},{24,32},{32,40},{40,48},{48,56},{56,64},{64,7... | collective-permute-start | bytes 24584 | tf_op jit(solution)/shard_map/ppermute | solution.py:31
  199.3 1.9 collective-permute-start.5
  202.0 6.6 collective-permute-done.5
  208.6 1.9 collective-permute-start.6
  210.5 3.5 collective-permute-start.7
  214.8 2.5 collective-permute-done.7
  219.2 54.8 %gather_fusion = f32[16384,2]{1,0:T(8,128)} fusion(f32[2,6336]{0,1:T(8,128)S(1)} %bitcast.222, s32[16384]{0:T(1024)S(1)} %get-tuple-element.538), kind=kCustom, calls=%fused_computation | custom fusion | bytes 327680 | tf_op jit(solution)/shard_map/gather | solution.py:210
  273.9 5.6 copy.116
  279.5 78.5 %while.61 = (s32[]{:T(128)}, f32[16,8,12,128]{3,1,0,2:T(8,128)S(1)}, f32[16,8,12,128]{3,1,0,2:T(8,128)}, f32[16,8,2,128]{3,2,1,0:T(2,128)S(1)}, s32[]{:T(128)}) while((s32[]{:T(128)}, f32[16,8,12,128]{3,1,0,2:T(8,128)S(1)}, f32[16,8,12,128]{3,1,0,2:T(8,128)}, f32[16,8,2,128]{3,2,1,0:T(2,128)S(1)}, s32[]{:T(128)}) %tuple.244), condition=%wide.region_4.5_spmd, body=%wide.region_3.4_spmd.sunk | while | flops 18522880 | bytes 516177 | solution.py:139
  359.3 3.1 collective-permute-start.8
  363.7 1.9 collective-permute-start.9
  367.4 6.5 collective-permute-done.9
  375.7 1.9 collective-permute-start.10
  379.0 3.4 collective-permute-start.11
  384.1 2.4 collective-permute-done.11
  387.7 48.7 %while.62 = (s32[]{:T(128)}, f32[16,8,5,128]{3,2,1,0:T(8,128)S(1)}, f32[16,8,12,128]{3,2,1,0:T(8,128)S(1)}, s32[]{:T(128)}) while((s32[]{:T(128)}, f32[16,8,5,128]{3,2,1,0:T(8,128)S(1)}, f32[16,8,12,128]{3,2,1,0:T(8,128)S(1)}, s32[]{:T(128)}) %tuple.238), condition=%wide.region_10.11_spmd, body=%wide.region_9.10_spmd.sunk | while | flops 20079360 | bytes 319549 | solution.py:139
  436.4 4.9 copy.124
  441.2 88.6 %scatter_custom_fusion.5 = f32[5,6336]{0,1:T(8,128)S(1)} fusion(s32[16384]{0:T(1024)S(1)} %bitcast.268, f32[16384,5]{1,0:T(8,128)} %bitcast.219, f32[]{:T(128)} %constant.678.clone.1), kind=kCustom, calls=%fused_computation.509 | custom fusion | flops 81920 | bytes 127232 | tf_op jit(solution)/shard_map/scatter-add | solution.py:189
  532.4 3.0 collective-permute-start.12
  536.9 2.6 copy.152
  542.1 1.9 collective-permute-start.13
  544.1 7.5 collective-permute-done.13
  551.7 1.9 collective-permute-start.14
  553.7 3.4 collective-permute-start.15
  557.5 3.1 collective-permute-done.15
  561.5 3.1 collective-permute-start.16
  564.6 1.9 collective-permute-start.17
  567.2 6.6 collective-permute-done.17
  573.9 1.9 collective-permute-start.18
  575.8 3.4 collective-permute-start.19
  584.5 54.8 %gather_fusion.7 = f32[16384,2]{1,0:T(8,128)} fusion(f32[2,6336]{0,1:T(8,128)S(1)} %bitcast.221, s32[16384]{0:T(1024)S(1)} %get-tuple-element.537), kind=kCustom, calls=%fused_computation.7 | custom fusion | bytes 327680 | tf_op jit(solution)/shard_map/gather | solution.py:210
  639.2 5.6 copy.130
  644.8 78.5 %while.63 = (s32[]{:T(128)}, f32[16,8,12,128]{3,1,2,0:T(8,128)S(1)}, f32[16,8,12,128]{3,1,2,0:T(8,128)}, f32[16,8,2,128]{3,2,1,0:T(2,128)S(1)}, s32[]{:T(128)}) while((s32[]{:T(128)}, f32[16,8,12,128]{3,1,2,0:T(8,128)S(1)}, f32[16,8,12,128]{3,1,2,0:T(8,128)}, f32[16,8,2,128]{3,2,1,0:T(2,128)S(1)}, s32[]{:T(128)}) %tuple.243), condition=%wide.region_13.14_spmd, body=%wide.region_12.13_spmd.sunk | while | flops 18522880 | bytes 516177 | solution.py:139
  724.1 3.1 collective-permute-start.20
  728.4 1.9 collective-permute-start.21
  731.9 6.7 collective-permute-done.21
  740.2 1.9 collective-permute-start.22
  743.4 3.4 collective-permute-start.23
  748.4 2.5 collective-permute-done.23
  (1037 shorter events, 315.5 us)
Async XLA Ops:
  67.4 101.3 %copy-start.19 = (s32[2,4,13,1,1]{2,4,3,1,0:T(1,128)S(1)}, s32[2,4,13,1,1]{2,4,3,1,0:T(1,128)}, u32[]{:S(2)}) copy-start(s32[2,4,13,1,1]{2,4,3,1,0:T(1,128)} %param.33) | copy-start | bytes 1252
  67.4 103.0 %copy-start.4 = (s32[2,4,1,1]{1,3,2,0:T(1,128)S(1)}, s32[2,4,1,1]{1,3,2,0:T(1,128)}, u32[]{:S(2)}) copy-start(s32[2,4,1,1]{1,3,2,0:T(1,128)} %param.32) | copy-start | bytes 100
  159.0 18.9 %collective-permute-start = (f32[5,4,264]{2,1,0:T(4,128)}, f32[5,4,264]{2,1,0:T(4,128)}, u32[]{:S(2)}, u32[]{:S(2)}) collective-permute-start(f32[5,4,264]{2,1,0:T(4,128)} %copy.150), channel_id=1, source_target_pairs={{0,8},{8,16},{16,24},{24,32},{32,40},{40,48},{48,56},{56,64},{64,7... | collective-permute-start | bytes 63368 | tf_op jit(solution)/shard_map/ppermute | solution.py:31
  166.6 12.1 %collective-permute-start.1 = (f32[5,4,264]{2,1,0:T(4,128)S(1)}, f32[5,4,264]{2,1,0:T(4,128)}, u32[]{:S(2)}, u32[]{:S(2)}) collective-permute-start(f32[5,4,264]{2,1,0:T(4,128)S(1)} %copy.151), channel_id=1, source_target_pairs={{8,0},{16,8},{24,16},{32,24},{40,32},{48,40},{56,48},{64,56},{72,6... | collective-permute-start | bytes 63368 | tf_op jit(solution)/shard_map/ppermute | solution.py:32
  169.3 3.1 copy-start.11
  169.3 3.1 copy-start.13
  169.3 3.1 copy-start.15
  169.3 3.1 copy-start.17
  169.3 8.6 %copy-start.7 = (s32[13]{0:T(128)}, s32[13]{0:T(128)S(1)}, u32[]{:S(2)}) copy-start(s32[13]{0:T(128)S(1)} %get-tuple-element.522) | copy-start | bytes 160
  169.3 12.8 %copy-start.9 = (s32[13]{0:T(128)}, s32[13]{0:T(128)S(1)}, u32[]{:S(2)}) copy-start(s32[13]{0:T(128)S(1)} %get-tuple-element.523) | copy-start | bytes 160
  179.5 5.4 collective-permute-start.2
  182.2 6.9 collective-permute-start.3
  190.1 11.8 %collective-permute-start.4 = (f32[2,4,256]{2,1,0:T(4,128)S(1)}, f32[2,4,256]{2,1,0:T(4,128)S(1)}, u32[]{:S(2)}, u32[]{:S(2)}) collective-permute-start(f32[2,4,256]{2,1,0:T(4,128)S(1)} %get-tuple-element.519), channel_id=1, source_target_pairs={{0,8},{8,16},{16,24},{24,32},{32,40},{40,48},{48,56},{56,64},{64,7... | collective-permute-start | bytes 24584 | tf_op jit(solution)/shard_map/ppermute | solution.py:31
  199.3 9.2 %collective-permute-start.5 = (f32[2,4,256]{2,1,0:T(4,128)S(1)}, f32[2,4,256]{2,1,0:T(4,128)S(1)}, u32[]{:S(2)}, u32[]{:S(2)}) collective-permute-start(f32[2,4,256]{2,1,0:T(4,128)S(1)} %get-tuple-element.520), channel_id=1, source_target_pairs={{8,0},{16,8},{24,16},{32,24},{40,32},{48,40},{56,48},{64,56},{72,6... | collective-permute-start | bytes 24584 | tf_op jit(solution)/shard_map/ppermute | solution.py:32
  208.6 6.1 collective-permute-start.6
  210.5 6.7 collective-permute-start.7
  273.9 5.6 copy-start.3
  279.5 86.2 %copy-start.18 = (s32[13]{0:T(128)S(1)}, s32[13]{0:T(128)}, u32[]{:S(2)}) copy-start(s32[13]{0:T(128)} %copy-done.17) | copy-start | bytes 160
  358.1 16.0 %copy-start.16 = (s32[13]{0:T(128)S(1)}, s32[13]{0:T(128)}, u32[]{:S(2)}) copy-start(s32[13]{0:T(128)} %copy-done.15) | copy-start | bytes 160
  358.1 24.4 %copy-start.14 = (s32[13]{0:T(128)S(1)}, s32[13]{0:T(128)}, u32[]{:S(2)}) copy-start(s32[13]{0:T(128)} %copy-done.13) | copy-start | bytes 160
  358.1 28.5 %copy-start.12 = (s32[13]{0:T(128)S(1)}, s32[13]{0:T(128)}, u32[]{:S(2)}) copy-start(s32[13]{0:T(128)} %copy-done.11) | copy-start | bytes 160
  359.3 6.4 collective-permute-start.8
  363.7 10.2 %collective-permute-start.9 = (f32[13,12,128]{2,1,0:T(8,128)S(1)}, f32[13,12,128]{2,1,0:T(8,128)S(1)}, u32[]{:S(2)}, u32[]{:S(2)}) collective-permute-start(f32[13,12,128]{2,1,0:T(8,128)S(1)} %gather_fusion.2), channel_id=1, source_target_pairs={{8,0},{16,8},{24,16},{32,24},{40,32},{48,40},{56,48},{64,56},{72,6... | collective-permute-start | bytes 239624 | tf_op jit(solution)/shard_map/ppermute | solution.py:32
  375.7 6.6 collective-permute-start.10
  379.0 7.6 %collective-permute-start.11 = (f32[13,12,128]{2,1,0:T(8,128)S(1)}, f32[13,12,128]{2,1,0:T(8,128)S(1)}, u32[]{:S(2)}, u32[]{:S(2)}) collective-permute-start(f32[13,12,128]{2,1,0:T(8,128)S(1)} %gather_fusion.5), channel_id=1, source_target_pairs={{1,0},{2,1},{3,2},{4,3},{5,4},{6,5},{7,6},{9,8},{10,9},{11,10},{12... | collective-permute-start | bytes 239624 | tf_op jit(solution)/shard_map/ppermute | solution.py:32
  436.3 4.9 copy-start
  441.2 94.1 %copy-start.5 = (s32[13]{0:T(128)S(1)}, s32[13]{0:T(128)}, u32[]{:S(2)}) copy-start(s32[13]{0:T(128)} %get-tuple-element.521) | copy-start | bytes 160
  532.4 11.7 %collective-permute-start.12 = (f32[5,4,264]{2,1,0:T(4,128)S(1)}, f32[5,4,264]{2,1,0:T(4,128)S(1)}, u32[]{:S(2)}, u32[]{:S(2)}) collective-permute-start(f32[5,4,264]{2,1,0:T(4,128)S(1)} %copy.154), channel_id=1, source_target_pairs={{0,8},{8,16},{16,24},{24,32},{32,40},{40,48},{48,56},{56,64},{64,7... | collective-permute-start | bytes 63368 | tf_op jit(solution)/shard_map/ppermute | solution.py:31
  535.4 18.2 %copy-start.6 = (s32[13]{0:T(128)S(1)}, s32[13]{0:T(128)}, u32[]{:S(2)}) copy-start(s32[13]{0:T(128)} %get-tuple-element.528) | copy-start | bytes 160
  536.9 42.9 %copy-start.1 = (f32[16,8,12,128]{3,2,1,0:T(8,128)S(1)}, f32[16,8,12,128]{3,2,1,0:T(8,128)}, u32[]{:S(2)}) copy-start(f32[16,8,12,128]{3,2,1,0:T(8,128)} %copy-done) | copy-start | bytes 2359300
  542.1 9.4 %collective-permute-start.13 = (f32[5,4,264]{2,1,0:T(4,128)S(1)}, f32[5,4,264]{2,1,0:T(4,128)S(1)}, u32[]{:S(2)}, u32[]{:S(2)}) collective-permute-start(f32[5,4,264]{2,1,0:T(4,128)S(1)} %copy.155), channel_id=1, source_target_pairs={{8,0},{16,8},{24,16},{32,24},{40,32},{48,40},{56,48},{64,56},{72,6... | collective-permute-start | bytes 63368 | tf_op jit(solution)/shard_map/ppermute | solution.py:32
  551.7 5.4 collective-permute-start.14
  553.7 6.9 collective-permute-start.15
  561.5 5.7 collective-permute-start.16
  564.6 9.2 %collective-permute-start.17 = (f32[2,4,256]{2,1,0:T(4,128)S(1)}, f32[2,4,256]{2,1,0:T(4,128)S(1)}, u32[]{:S(2)}, u32[]{:S(2)}) collective-permute-start(f32[2,4,256]{2,1,0:T(4,128)S(1)} %get-tuple-element.518), channel_id=1, source_target_pairs={{8,0},{16,8},{24,16},{32,24},{40,32},{48,40},{56,48},{64,56},{72,6... | collective-permute-start | bytes 24584 | tf_op jit(solution)/shard_map/ppermute | solution.py:32
  573.9 7.1 collective-permute-start.18
  575.8 6.7 collective-permute-start.19
  639.2 5.6 copy-start.2
  644.8 85.6 %copy-start.10 = (s32[13]{0:T(128)S(1)}, s32[13]{0:T(128)}, u32[]{:S(2)}) copy-start(s32[13]{0:T(128)} %copy-done.9) | copy-start | bytes 160
  723.4 15.3 %copy-start.8 = (s32[13]{0:T(128)S(1)}, s32[13]{0:T(128)}, u32[]{:S(2)}) copy-start(s32[13]{0:T(128)} %copy-done.7) | copy-start | bytes 160
  724.1 6.2 collective-permute-start.20
  728.4 10.2 %collective-permute-start.21 = (f32[13,12,128]{2,1,0:T(8,128)S(1)}, f32[13,12,128]{2,1,0:T(8,128)S(1)}, u32[]{:S(2)}, u32[]{:S(2)}) collective-permute-start(f32[13,12,128]{2,1,0:T(8,128)S(1)} %gather_fusion.9), channel_id=1, source_target_pairs={{8,0},{16,8},{24,16},{32,24},{40,32},{48,40},{56,48},{64,56},{72,6... | collective-permute-start | bytes 239624 | tf_op jit(solution)/shard_map/ppermute | solution.py:32
  740.2 6.5 collective-permute-start.22
  743.4 7.6 %collective-permute-start.23 = (f32[13,12,128]{2,1,0:T(8,128)S(1)}, f32[13,12,128]{2,1,0:T(8,128)S(1)}, u32[]{:S(2)}, u32[]{:S(2)}) collective-permute-start(f32[13,12,128]{2,1,0:T(8,128)S(1)} %gather_fusion.12), channel_id=1, source_target_pairs={{1,0},{2,1},{3,2},{4,3},{5,4},{6,5},{7,6},{9,8},{10,9},{11,10},{12... | collective-permute-start | bytes 239624 | tf_op jit(solution)/shard_map/ppermute | solution.py:32
where the time goes:
time: 757 us; the launch traced here: 753 us
  matrix products  217 us (29%)
  local copies, waits for them, and re-layouts  216 us (29%)
  other arithmetic  193 us (25%)
  starting transfers between devices  71.1 us (9%)
  waiting for transfers between devices  49.7 us (7%)
    scatter-add x2, other arithmetic, on_device(): node_sums = jnp.zeros((5, grid_height * grid_width), jnp.float32).at[:, f...  177 us
    gather x2, local copies, waits for them, and re-layouts, on_device(): window_grid.reshape(2, -1)[:, flat_index]  110 us
    ppermute x12, waiting for transfers between devices, padded(): after = lax.ppermute(initial, axis, down)  49.6 us
    dot_general x32, matrix products, gather_terms(): jnp.einsum('bcn,bpn->bcp', window_vel, grad_cross, precision=HIGHEST)  41.3 us
    dot_general x32, matrix products, gather_terms(): jnp.einsum('bcn,bpn->bcp', window_vel, grad_down, precision=HIGHEST)  41.3 us
    dot_general x32, matrix products, gather_terms(): jnp.einsum('bcn,bpn->bcp', window_vel, weight, precision=HIGHEST)  41.1 us
    ppermute x12, starting transfers between devices, padded(): before = lax.ppermute(last, axis, up)  39.9 us
    dot_general x32, matrix products, scatter_terms(): jnp.einsum('bcp,bpn->bcn', stress_cross, grad_cross, precision=HIGHEST)  31.4 us
  transfers between devices with their start and end apart: 24, of which 11 were waited for; matrix products, arithmetic and copies ran while one was open for 5% of the time, Pallas kernels for 0%

commit v1 on v0

v1 whole, which is shorter than its diff:
```python
import jax
import jax.numpy as jnp
from jax import lax
from jax.experimental import pallas as pl
from jax.experimental.pallas import tpu as pltpu
from jax.sharding import PartitionSpec as P

WIN_DOWN = 8
WIN_CROSS = 16
GHOST = 4
STEPS = 2
MOVE_CAP = 13
TILE_DOWN = 16
TILE_CROSS = 256
BLOCKS = 128
FIELDS = 12
LANES = 128
TIME_STEP = 0.1
GRAVITY = 5.6
MASS_FLOOR = 0.5

F32 = jnp.float32
BF16 = jnp.bfloat16
MESH = pl.DeviceIdType.MESH

COLS = 272
BAND = 40
SPAN = 32
PAD = COLS - SPAN
CHUNK = 96
PITCH = 16
SLOTS = 16
OUT_ROWS = 4 * SLOTS * PITCH
ALL_ROWS = BLOCKS * PITCH
SEND_ROWS = MOVE_CAP * PITCH
STRIDE_PAD = 16
ORDER_0, ORDER_1, SOURCE_1, PLACE_1 = range(4)

NEAR = ((-1, 0), (1, 0), (0, -1), (0, 1), (-1, -1), (1, -1), (-1, 1), (1, 1))
MOVES = ((1, 0), (-1, 0), (0, 1), (0, -1))


def spline_pair(distance):
    magnitude = jnp.abs(distance)
    outer = jnp.maximum(1.5 - magnitude, 0.0)
    inner = jnp.maximum(0.5 - magnitude, 0.0)
    inner3 = 3.0 * inner
    value = 0.5 * (outer * outer - inner3 * inner)
    steep = outer - inner3
    return value, jnp.where(distance > 0.0, -steep, steep)


def split(x):
    high = x.astype(BF16)
    return high, (x - high.astype(F32)).astype(BF16)


def matmul_t(a, b):
    return lax.dot_general(a, b, (((1,), (1,)), ((), ())), preferred_element_type=F32)


def sum_rows(parts, sublane):
    half = []
    for k in range(4):
        a, b = parts[k], parts[k + 4]
        low = sublane < 4
        half.append(jnp.where(low, a, b) + pltpu.roll(jnp.where(low, b, a), 4, 0))
    quarter = []
    for k in range(2):
        a, b = half[k], half[k + 2]
        a = a + pltpu.roll(a, 6, 0)
        b = b + pltpu.roll(b, 2, 0)
        quarter.append(jnp.where(sublane % 4 < 2, a, b))
    a, b = quarter
    a = a + pltpu.roll(a, 7, 0)
    b = b + pltpu.roll(b, 1, 0)
    return jnp.where(sublane % 2 == 0, a, b)


def kernel(
    tables,
    anchor_down,
    anchor_cross,
    count,
    particles,
    result,
    stage,
    rows_kept,
    cols_kept,
    spread,
    grid,
    pack,
    row_in,
    col_in,
    window,
    leaving,
    arrived,
    state_1,
    state_2,
    halo_send,
    halo_recv,
    move_send,
    move_recv,
):
    flat_1 = state_1.reshape(ALL_ROWS + STRIDE_PAD, LANES)
    flat_2 = state_2.reshape(ALL_ROWS + STRIDE_PAD, LANES)
    size_down, size_cross = lax.axis_size("down"), lax.axis_size("cross")
    me_down, me_cross = lax.axis_index("down"), lax.axis_index("cross")

    def at(step):
        return (
            lax.rem(me_down + step[0] + size_down, size_down),
            lax.rem(me_cross + step[1] + size_cross, size_cross),
        )

    barrier = pltpu.get_barrier_semaphore()
    for step in NEAR:
        pl.semaphore_signal(barrier, inc=1, device_id=at(step), device_id_type=MESH)

    sublane = lax.broadcasted_iota(jnp.int32, (8, LANES), 0)
    lane8 = lax.broadcasted_iota(jnp.int32, (8, LANES), 1)
    row_number = lax.broadcasted_iota(jnp.int32, (24, LANES), 0).astype(F32)
    col_number = lax.broadcasted_iota(jnp.int32, (SPAN, LANES), 0).astype(F32)
    no_terms = jnp.zeros((BAND - 16, LANES), F32)
    no_tail = jnp.zeros((8, LANES), F32)

    for k in range(8):
        spread[k] = jnp.zeros(((PAD + SPAN + PAD) // 8, 8, LANES), F32)

    def strided(ref, first, field):
        return ref[pl.ds(first + field, 8, stride=PITCH), :]

    def slot_of(step, block):
        return block if step == 0 else tables[ORDER_0, block]

    def scatter(step, batch, fields):
        u, w, v_down, v_cross, s_dd, s_dc, s_cc, mass, volume = fields[:9]
        less = -volume
        values = [mass, mass * v_down, mass * v_cross, less * s_dd, less * s_dc, less * s_cc]
        bases = []
        for k in range(8):
            block = batch * 8 + k
            slot = slot_of(step, block)
            first_row = anchor_down[step, slot] + GHOST
            first_col = anchor_cross[step, slot] + GHOST
            group = lax.shift_right_logical(first_col, 4)
            bases.append(PAD // 8 - 2 * group)
            row_shift = first_row.astype(F32)
            col_shift = (first_col - 16 * group).astype(F32)
            r_value, r_slope = spline_pair(u[k : k + 1] - (row_number - row_shift))
            c_value, c_slope = spline_pair(w[k : k + 1] - (col_number - col_shift))
            c_high, c_low = split(c_value)
            d_high, d_low = split(c_slope)
            rows_kept[block] = jnp.concatenate([r_value, r_slope], axis=0)
            cols_kept[block, :, :LANES] = jnp.concatenate([c_high, c_low], axis=0)
            cols_kept[block, :, LANES:] = jnp.concatenate([d_high, d_low], axis=0)
            m, md, mc, dd, dc, cc = (x[k : k + 1] for x in values)
            first, second = [], []
            for g in range(3):
                r, s = r_value[8 * g : 8 * g + 8], r_slope[8 * g : 8 * g + 8]
                first += [r * m, r * md, r * mc, s * dd, s * dc]
                second += [no_terms, r * dc, r * cc]
            a_high, a_low = split(jnp.concatenate(first + [no_tail], axis=0))
            b_high, b_low = split(jnp.concatenate(second + [no_tail], axis=0))
            left = jnp.concatenate([c_high, c_low, c_high, d_high, d_low, d_high], axis=1)
            right = jnp.concatenate([a_high, a_high, a_low, b_high, b_high, b_low], axis=1)
            sums = matmul_t(left, right)
            for v in range(SPAN // 8):
                spread[k, PAD // 8 + v] = sums[8 * v : 8 * v + 8]
        for v in range(COLS // 8):
            total = grid[step, 8 * v : 8 * v + 8, :]
            for k in range(8):
                total = total + spread[k, bases[k] + v]
            grid[step, 8 * v : 8 * v + 8, :] = total

    def gather(step, batch, load_block, order, target, first):
        parts = [[] for _ in range(6)]
        for k in range(8):
            position = batch * 8 + k
            slot = tables[order, position]
            block = slot if step == 0 else tables[SOURCE_1, position]
            group = lax.shift_right_logical(anchor_cross[step, slot] + GHOST, 4)
            cols = cols_kept[block]
            moved = lax.dot_general(
                window[group],
                jnp.concatenate([cols, cols], axis=0),
                (((1,), (0,)), ((), ())),
                preferred_element_type=F32,
            )
            rows = rows_kept[block]
            sums = [None] * 6
            for g in range(3):
                r, s = rows[8 * g : 8 * g + 8], rows[24 + 8 * g : 32 + 8 * g]
                down, cross = moved[16 * g : 16 * g + 8], moved[16 * g + 8 : 16 * g + 16]
                terms = [
                    r * down[:, :LANES],
                    r * cross[:, :LANES],
                    s * down[:, :LANES],
                    s * cross[:, :LANES],
                    r * down[:, LANES:],
                    r * cross[:, LANES:],
                ]
                sums = [t if a is None else a + t for a, t in zip(sums, terms)]
            for held, total in zip(parts, sums):
                held.append(total)
            load_block(k, block)
        new_down, new_cross, l_dd, l_cd, l_dc, l_cc = (sum_rows(p, sublane) for p in parts)
        f = [strided(stage, 0, i) for i in range(FIELDS)]
        rate_dc = 0.5 * (l_dc + l_cd)
        trace = l_dd + l_cc
        shear, lame = f[9], f[10]
        updated = [
            jnp.clip(f[0] + TIME_STEP * new_down, 0.5, WIN_DOWN - 1.5),
            jnp.clip(f[1] + TIME_STEP * new_cross, 0.5, WIN_CROSS - 1.5),
            new_down,
            new_cross,
            f[4] + TIME_STEP * (lame * trace + 2.0 * shear * l_dd),
            f[5] + TIME_STEP * (2.0 * shear * rate_dc),
            f[6] + TIME_STEP * (lame * trace + 2.0 * shear * l_cc),
            f[7],
            f[8] * (1.0 + TIME_STEP * trace),
            shear,
            lame,
            f[11] + TIME_STEP * (l_dd * l_dd + l_cc * l_cc + 2.0 * rate_dc * rate_dc),
        ]
        for i, x in enumerate(updated):
            target[pl.ds(first + i, 8, stride=PITCH), :] = x

    def remote(source, target, send, recv, step):
        return pltpu.make_async_remote_copy(
            src_ref=source,
            dst_ref=target,
            send_sem=send,
            recv_sem=recv,
            device_id=at(step),
            device_id_type=MESH,
        )

    lane = lax.broadcasted_iota(jnp.int32, (CHUNK, LANES), 1)

    def placed(parts, shifts):
        out = [pltpu.roll(p, s, 1) if s else p for p, s in zip(parts, shifts)]
        where = lane[: out[0].shape[0]]
        if len(out) == 2:
            return jnp.where(where < BAND, out[0], out[1])
        return jnp.where(where < BAND, out[0], jnp.where(where < 2 * BAND, out[1], out[2]))

    def exchange(step):
        short = COLS - 2 * CHUNK
        a, b = grid[step, :CHUNK, :], grid[step, CHUNK : 2 * CHUNK, :]
        c = grid[step, 2 * CHUNK :, :]
        for side, shifts in enumerate(((0, 40, 80), (48, 88, 0))):
            pack[step, side, :short] = placed([a[:short], b[:short], c], shifts)
            pack[step, side, short:] = placed([a[short:], b[short:]], shifts[:2])
        first = grid.at[step, pl.ds(0, 8), :]
        last = grid.at[step, pl.ds(TILE_CROSS, 8), :]
        copies = []
        for n, (near, source, target) in enumerate(
            (
                ((-1, 0), pack.at[step, 0], row_in.at[step, 1]),
                ((1, 0), pack.at[step, 1], row_in.at[step, 0]),
                ((0, -1), first, col_in.at[step, 1]),
                ((0, 1), last, col_in.at[step, 0]),
                ((-1, -1), first, col_in.at[step, 5]),
                ((1, -1), first, col_in.at[step, 4]),
                ((-1, 1), last, col_in.at[step, 3]),
                ((1, 1), last, col_in.at[step, 2]),
            )
        ):
            copy = remote(source, target, halo_send.at[step, n], halo_recv.at[step, n], near)
            copy.start()
            copies.append(copy)
        return copies

    def velocities(step):
        above = me_down > 0
        below = me_down < size_down - 1
        before = me_cross > 0
        after = me_cross < size_cross - 1

        def keep(condition, mask, x):
            return jnp.where(mask & condition, x, 0.0)

        lane_1 = lane8
        low = lane_1 < BAND
        high = (lane_1 >= 2 * BAND) & (lane_1 < 3 * BAND)
        channel = lax.rem(lane_1, BAND) // 8
        row = 8 * (lane_1 // BAND) + lax.rem(lane_1, 8)
        row_global = me_down * TILE_DOWN - GHOST + row
        used = ((channel == 1) | (channel == 2)) & (lane_1 < 3 * BAND)
        row_keep = used & (row_global > 0) & (row_global < TILE_DOWN * size_down - 1)
        is_down = channel == 1
        pull = jnp.where(is_down, GRAVITY, 0.0)
        out = []
        for v in range(COLS // 8):
            total = grid[step, 8 * v : 8 * v + 8, :]
            part, inner = divmod(8 * v, CHUNK)
            from_above = row_in[step, 0, inner : inner + 8, :]
            from_below = row_in[step, 1, inner : inner + 8, :]
            turn = (LANES - BAND * part) % LANES
            total = total + keep(above, low, pltpu.roll(from_above, turn, 1) if turn else from_above)
            turn = (2 * BAND - BAND * part) % LANES
            total = total + keep(below, high, pltpu.roll(from_below, turn, 1) if turn else from_below)
            side = {0: (0, before, 2, 3), TILE_CROSS // 8: (1, after, 4, 5)}.get(v)
            if side:
                straight, there, up, down = side
                total = total + jnp.where(there, col_in[step, straight], 0.0)
                total = total + keep(there & above, low, pltpu.roll(col_in[step, up], 48, 1))
                total = total + keep(there & below, high, pltpu.roll(col_in[step, down], 80, 1))
            mass_down = pltpu.roll(total, 8, 1)
            mass = jnp.where(is_down, mass_down, pltpu.roll(total, 16, 1))
            force = pltpu.roll(total, LANES - 16, 1)
            moved = total + TIME_STEP * (force + pull * mass_down)
            col_global = me_cross * TILE_CROSS - GHOST + 8 * v + sublane
            inside = row_keep & (col_global > 0) & (col_global < TILE_CROSS * size_cross - 1)
            out.append(jnp.where(inside, moved / jnp.maximum(mass, MASS_FLOOR), 0.0))
        out += [no_tail] * (3 * LANES // 8 - len(out))
        turned = []
        for t in range(3):
            block = jnp.concatenate(out[16 * t : 16 * t + 16], axis=0).T
            turned.append(
                jnp.concatenate([block[BAND * g + 8 : BAND * g + 24] for g in range(3)], axis=0)
            )
        turned = jnp.concatenate(turned, axis=1)
        top = turned.astype(BF16).astype(F32)
        rest = turned - top
        for g in range(16):
            a, b = top[:, 16 * g : 16 * g + SPAN], rest[:, 16 * g : 16 * g + SPAN]
            window[g] = jnp.concatenate([a, a, b, b], axis=1).astype(BF16)

    def wait_all(copies):
        for copy in copies:
            copy.wait()

    def send_blocks(step):
        copies = []
        for k, near in enumerate(MOVES):
            copy = remote(
                leaving.at[step, pl.ds(k * SLOTS * PITCH, SEND_ROWS), :],
                arrived.at[step, pl.ds((k ^ 1) * SLOTS * PITCH, SEND_ROWS), :],
                move_send.at[step, k],
                move_recv.at[step, k],
                near,
            )
            copy.start()
            copies.append(copy)
        return copies

    for step in range(STEPS):
        grid[step] = jnp.zeros((COLS, LANES), F32)

    def scatter_0(batch, carry):
        for k in range(8):
            stage[PITCH * k : PITCH * k + FIELDS, :] = particles[batch * 8 + k]
        scatter(0, batch, [strided(stage, 0, i) for i in range(FIELDS)])
        return carry

    lax.fori_loop(0, BLOCKS // 8, scatter_0, 0)
    pl.semaphore_wait(barrier, len(NEAR))
    wait_all(exchange(0))
    velocities(0)

    def load_0(k, block):
        stage[PITCH * k : PITCH * k + FIELDS, :] = particles[block]

    def gather_leaving_0(batch, carry):
        gather(0, batch, load_0, ORDER_0, leaving.at[0], batch * 8 * PITCH)
        return carry

    def gather_staying_0(batch, carry):
        gather(0, batch, load_0, ORDER_0, flat_1, batch * 8 * PITCH)
        return carry

    lax.fori_loop(0, 8, gather_leaving_0, 0)
    copies = send_blocks(0)
    lax.fori_loop(8, 16, gather_staying_0, 0)

    def scatter_staying(batch, carry):
        scatter(1, batch, [strided(flat_1, batch * 8 * PITCH, i) for i in range(FIELDS)])
        return carry

    def scatter_arrived(batch, carry):
        first = batch * 8 * PITCH
        here = (lax.rem(batch, 2) * 8 + sublane) < count[0, batch // 2]
        fields = [
            jnp.where(here, strided(arrived.at[0], first, i), strided(leaving.at[0], first, i))
            for i in range(FIELDS)
        ]
        for i, x in enumerate(fields):
            flat_1[pl.ds(first + i, 8, stride=PITCH), :] = x
        scatter(1, batch, fields)
        return carry

    lax.fori_loop(8, 16, scatter_staying, 0)
    wait_all(copies)
    lax.fori_loop(0, 8, scatter_arrived, 0)
    wait_all(exchange(1))
    velocities(1)

    def load_1(k, block):
        stage[PITCH * k : PITCH * k + FIELDS, :] = state_1[block, :FIELDS, :]

    def gather_leaving_1(batch, carry):
        gather(1, batch, load_1, ORDER_1, leaving.at[1], batch * 8 * PITCH)
        return carry

    def gather_staying_1(batch, carry):
        gather(1, batch, load_1, ORDER_1, flat_2, batch * 8 * PITCH)
        return carry

    lax.fori_loop(0, 8, gather_leaving_1, 0)
    copies = send_blocks(1)
    lax.fori_loop(8, 16, gather_staying_1, 0)
    wait_all(copies)

    def settle(block, carry):
        here = jnp.full((PITCH, LANES), lax.rem(block, SLOTS)) < count[1, block // SLOTS]
        rows = pl.ds(pl.multiple_of(block * PITCH, PITCH), PITCH)
        state_2[block] = jnp.where(here, arrived[1, rows, :], leaving[1, rows, :])
        return carry

    lax.fori_loop(0, 4 * SLOTS, settle, 0, unroll=4)

    def put(slot, carry):
        place = tables[PLACE_1, slot]
        result[slot] = state_2[place, :FIELDS, :]
        return carry

    lax.fori_loop(0, BLOCKS, put, 0, unroll=4)


def slot_tables(move_slots):
    listed = jnp.pad(
        move_slots[:, :, :, 0, 0], ((0, 0), (0, 0), (0, SLOTS - MOVE_CAP)), constant_values=-1
    ).reshape(STEPS, 4 * SLOTS, 1)
    slot = jnp.arange(BLOCKS, dtype=jnp.int32)
    same = listed == slot
    position = jnp.arange(4 * SLOTS, dtype=jnp.int32)[:, None]
    used = jnp.sum(same.astype(jnp.int32), axis=1)
    there = jnp.sum(jnp.where(same, position, 0), axis=1)
    earlier = jnp.sum(((listed >= 0) & (listed < slot)).astype(jnp.int32), axis=1)
    rank = slot - earlier
    spare = 4 * (SLOTS - MOVE_CAP)
    third = rank // (SLOTS - MOVE_CAP)
    free = jnp.where(
        rank < spare,
        SLOTS * third + MOVE_CAP + rank - (SLOTS - MOVE_CAP) * third,
        4 * MOVE_CAP + rank,
    )
    place = jnp.where(used > 0, there, free)
    held = place[:, None, :] == slot[None, :, None]
    order = jnp.sum(jnp.where(held, slot, 0), axis=2)
    source = jnp.sum(jnp.where(held[1], place[0], 0), axis=1)
    return jnp.stack([order[0], order[1], source, place[1]])


def on_device(particles, anchor_down, anchor_cross, move_count, move_slots):
    smem = pl.BlockSpec(memory_space=pltpu.SMEM)
    vmem = pl.BlockSpec(memory_space=pltpu.VMEM)
    return pl.pallas_call(
        kernel,
        out_shape=jax.ShapeDtypeStruct(particles.shape, F32),
        in_specs=[smem, smem, smem, smem, vmem],
        out_specs=vmem,
        scratch_shapes=[
            pltpu.VMEM((8 * PITCH + STRIDE_PAD, LANES), F32),
            pltpu.VMEM((BLOCKS, 48, LANES), F32),
            pltpu.VMEM((BLOCKS, 2 * SPAN, 2 * LANES), BF16),
            pltpu.VMEM((8, (PAD + SPAN + PAD) // 8, 8, LANES), F32),
            pltpu.VMEM((STEPS, COLS, LANES), F32),
            pltpu.VMEM((STEPS, 2, CHUNK, LANES), F32),
            pltpu.VMEM((STEPS, 2, CHUNK, LANES), F32),
            pltpu.VMEM((STEPS, 6, 8, LANES), F32),
            pltpu.VMEM((16, 48, LANES), BF16),
            pltpu.VMEM((STEPS, OUT_ROWS + STRIDE_PAD, LANES), F32),
            pltpu.VMEM((STEPS, OUT_ROWS + STRIDE_PAD, LANES), F32),
            pltpu.VMEM((BLOCKS + 1, PITCH, LANES), F32),
            pltpu.VMEM((BLOCKS + 1, PITCH, LANES), F32),
            pltpu.SemaphoreType.DMA((STEPS, 8)),
            pltpu.SemaphoreType.DMA((STEPS, 8)),
            pltpu.SemaphoreType.DMA((STEPS, 4)),
            pltpu.SemaphoreType.DMA((STEPS, 4)),
        ],
        compiler_params=pltpu.CompilerParams(
            collective_id=0, has_side_effects=True, vmem_limit_bytes=40 * 1024 * 1024
        ),
    )(
        slot_tables(move_slots),
        anchor_down,
        anchor_cross,
        move_count[:, :, 0, 0],
        particles,
    )


def solution(mesh):
    return jax.shard_map(
        on_device,
        mesh=mesh,
        in_specs=(
            P(("down", "cross"), None, None),
            P(None, ("down", "cross")),
            P(None, ("down", "cross")),
            P(None, None, "down", "cross"),
            P(None, None, None, "down", "cross"),
        ),
        out_specs=P(("down", "cross"), None, None),
        check_vma=False,
    )
```

time: 757 us -> 65.3 us (0.09)
  the two profiles are of different devices: /device:TPU:95 before, /device:TPU:6 now
where the time goes in v1:
time: 65.3 us; the launch traced here: 65 us
  Pallas kernels  61 us (93%)
  local copies, waits for them, and re-layouts  3.54 us (5%)
    pallas_call x1, Pallas kernels, on_device(): pl.pallas_call(kernel, out_shape=jax.ShapeDtypeStruct(particles.shape, F3...  61 us
    unnamed x7, local copies, waits for them, and re-layouts  1.64 us

profile of v1, /device:TPU:6, one launch (start us, length us, event | category | flops | bytes accessed | tf_op | source)
XLA Modules:
  0.0 65.0 jit_solution(1715257391699954844)
XLA Ops:
  0.0 0.7 %pad.4 = s32[2,4,16]{2,1,0:T(4,128)S(1)} pad(s32[2,4,13]{2,1,0:T(4,128)} %bitcast.10, s32[]{:T(128)} %constant.8.clone.1), padding=0_0x0_0x0_3 | pad | bytes 932 | tf_op jit(solution)/shard_map/jit(_pad)/pad | solution.py:433
  0.7 0.1 eq.30
  0.8 0.1 convert_reduce_fusion
  0.9 0.1 select_reduce_fusion
  1.1 0.1 select_reduce_fusion.1
  1.2 0.0 copy-start
  1.2 0.0 copy-start.1
  1.2 0.0 copy-start.2
  1.2 1.6 %copy.8.particles = f32[128,12,128]{2,1,0:T(8,128)S(1)} copy(f32[128,12,128]{2,0,1:T(8,128)} %param.5) | data formatting | bytes 1572864 | tf_op args[0]
  2.9 0.0 copy-done
  2.9 0.0 copy-done.1
  2.9 0.0 copy-done.2
  2.9 61.0 %shard_map.55 = f32[128,12,128]{2,1,0:T(8,128)S(1)} custom-call(s32[4,128]{1,0:T(4,128)S(1)} %pad_add_fusion.tables, s32[2,128]{1,0:T(2,128)S(1)} %copy-done, s32[2,128]{1,0:T(2,128)S(1)} %copy-done.1, s32[2,4]{1,0:T(2,128)S(1)} %bitcast.9, f32[128,12,128]{2,1,0:T(8,128)S(1)} %copy.8.particles), custom_call_target="tpu_custom_call" | custom-call | tf_op jit(solution)/shard_map/pallas_call | solution.py:460
  63.9 1.1 %copy.9 = f32[128,12,128]{2,0,1:T(8,128)} copy(f32[128,12,128]{2,1,0:T(8,128)S(1)} %shard_map.55) | data formatting | bytes 1572864 | tf_op jit(solution)/shard_map/pallas_call | solution.py:460
  (5 shorter events, 0.1 us)
Async XLA Ops:
  1.2 1.7 %copy-start = (s32[2,128]{1,0:T(2,128)S(1)}, s32[2,128]{1,0:T(2,128)}, u32[]{:S(2)}) copy-start(s32[2,128]{1,0:T(2,128)} %anchor_down.1) | copy-start | bytes 3076
  1.2 1.7 %copy-start.1 = (s32[2,128]{1,0:T(2,128)S(1)}, s32[2,128]{1,0:T(2,128)}, u32[]{:S(2)}) copy-start(s32[2,128]{1,0:T(2,128)} %anchor_cross.1) | copy-start | bytes 3076
  1.2 1.7 %copy-start.2 = (s32[2,4,1,1]{1,3,2,0:T(1,128)S(1)}, s32[2,4,1,1]{1,3,2,0:T(1,128)}, u32[]{:S(2)}) copy-start(s32[2,4,1,1]{1,3,2,0:T(1,128)} %param.8) | copy-start | bytes 100

commit v2 on v1

v2 whole, which is shorter than its diff:
```python
import jax
import jax.numpy as jnp
from jax import lax
from jax.experimental import pallas as pl
from jax.experimental.pallas import tpu as pltpu
from jax.sharding import PartitionSpec as P

WIN_DOWN = 8
WIN_CROSS = 16
GHOST = 4
STEPS = 2
MOVE_CAP = 13
TILE_DOWN = 16
TILE_CROSS = 256
BLOCKS = 128
FIELDS = 12
LANES = 128
TIME_STEP = 0.1
GRAVITY = 5.6
MASS_FLOOR = 0.5

F32 = jnp.float32
BF16 = jnp.bfloat16
MESH = pl.DeviceIdType.MESH

COLS = 272
BAND = 40
SPAN = 32
PAD = COLS - SPAN
PITCH = 16
SLOTS = 16
OUT_ROWS = 4 * SLOTS * FIELDS
ALL_ROWS = BLOCKS * PITCH
SEND_ROWS = 8 * -(-MOVE_CAP * FIELDS // 8)
STRIDE_PAD = 16
LOADS = 4
ORDER_0, ORDER_1, SOURCE_1, PLACE_1 = range(4)

NEAR = ((-1, 0), (1, 0), (0, -1), (0, 1), (-1, -1), (1, -1), (-1, 1), (1, 1))
MOVES = ((1, 0), (-1, 0), (0, 1), (0, -1))


def spline_pair(distance):
    magnitude = jnp.abs(distance)
    outer = jnp.maximum(1.5 - magnitude, 0.0)
    inner = jnp.maximum(0.5 - magnitude, 0.0)
    inner3 = 3.0 * inner
    value = 0.5 * (outer * outer - inner3 * inner)
    steep = outer - inner3
    return value, jnp.where(distance > 0.0, -steep, steep)


def split(x):
    high = x.astype(BF16)
    return high, (x - high.astype(F32)).astype(BF16)


def matmul_t(a, b):
    return lax.dot_general(a, b, (((1,), (1,)), ((), ())), preferred_element_type=F32)


def sum_rows(parts, sublane):
    half = []
    for k in range(4):
        a, b = parts[k], parts[k + 4]
        low = sublane < 4
        half.append(jnp.where(low, a, b) + pltpu.roll(jnp.where(low, b, a), 4, 0))
    quarter = []
    for k in range(2):
        a, b = half[k], half[k + 2]
        a = a + pltpu.roll(a, 6, 0)
        b = b + pltpu.roll(b, 2, 0)
        quarter.append(jnp.where(sublane % 4 < 2, a, b))
    a, b = quarter
    a = a + pltpu.roll(a, 7, 0)
    b = b + pltpu.roll(b, 1, 0)
    return jnp.where(sublane % 2 == 0, a, b)


def kernel(
    tables,
    anchor_down,
    anchor_cross,
    count,
    fields_hbm,
    result,
    fields_in,
    stage,
    rows_kept,
    cols_kept,
    spread,
    grid,
    turned,
    band_in,
    col_in,
    window,
    leaving,
    arrived,
    state_0,
    state_1,
    state_2,
    halo_send,
    halo_recv,
    move_send,
    move_recv,
    load_sem,
):
    flat_0 = state_0.reshape(ALL_ROWS + STRIDE_PAD, LANES)
    flat_1 = state_1.reshape(ALL_ROWS + STRIDE_PAD, LANES)
    flat_2 = state_2.reshape(ALL_ROWS + STRIDE_PAD, LANES)
    size_down, size_cross = lax.axis_size("down"), lax.axis_size("cross")
    me_down, me_cross = lax.axis_index("down"), lax.axis_index("cross")

    def at(step):
        return (
            lax.rem(me_down + step[0] + size_down, size_down),
            lax.rem(me_cross + step[1] + size_cross, size_cross),
        )

    loads = []
    for n in range(LOADS):
        part = pl.ds(n * BLOCKS // LOADS, BLOCKS // LOADS)
        loads.append(
            pltpu.make_async_copy(
                fields_hbm.at[:, part, :], fields_in.at[:, part, :], load_sem.at[n]
            )
        )
        loads[n].start()

    barrier = pltpu.get_barrier_semaphore()
    for step in NEAR:
        pl.semaphore_signal(barrier, inc=1, device_id=at(step), device_id_type=MESH)

    sublane = lax.broadcasted_iota(jnp.int32, (8, LANES), 0)
    lane8 = lax.broadcasted_iota(jnp.int32, (8, LANES), 1)
    row_number = lax.broadcasted_iota(jnp.int32, (24, LANES), 0).astype(F32)
    col_number = lax.broadcasted_iota(jnp.int32, (SPAN, LANES), 0).astype(F32)
    no_terms = jnp.zeros((BAND - 16, LANES), F32)
    no_tail = jnp.zeros((8, LANES), F32)

    for k in range(8):
        spread[k] = jnp.zeros(((PAD + SPAN + PAD) // 8, 8, LANES), F32)

    def strided(ref, first, pitch):
        return [ref[pl.ds(first + i, 8, stride=pitch), :] for i in range(FIELDS)]

    def put_strided(ref, first, pitch, fields):
        for i, x in enumerate(fields):
            ref[pl.ds(first + i, 8, stride=pitch), :] = x

    def slot_of(step, block):
        return block if step == 0 else tables[ORDER_0, block]

    def scatter(step, batch, fields):
        u, w, v_down, v_cross, s_dd, s_dc, s_cc, mass, volume = fields[:9]
        less = -volume
        values = [mass, mass * v_down, mass * v_cross, less * s_dd, less * s_dc, less * s_cc]
        bases = []
        for k in range(8):
            block = batch * 8 + k
            slot = slot_of(step, block)
            first_row = anchor_down[step, slot] + GHOST
            first_col = anchor_cross[step, slot] + GHOST
            group = lax.shift_right_logical(first_col, 4)
            bases.append(PAD // 8 - 2 * group)
            row_shift = first_row.astype(F32)
            col_shift = (first_col - 16 * group).astype(F32)
            r_value, r_slope = spline_pair(u[k : k + 1] - (row_number - row_shift))
            c_value, c_slope = spline_pair(w[k : k + 1] - (col_number - col_shift))
            c_high, c_low = split(c_value)
            d_high, d_low = split(c_slope)
            rows_kept[block] = jnp.concatenate([r_value, r_slope], axis=0)
            cols_kept[block, :, :LANES] = jnp.concatenate([c_high, c_low], axis=0)
            cols_kept[block, :, LANES:] = jnp.concatenate([d_high, d_low], axis=0)
            m, md, mc, dd, dc, cc = (x[k : k + 1] for x in values)
            first, second = [], []
            for g in range(3):
                r, s = r_value[8 * g : 8 * g + 8], r_slope[8 * g : 8 * g + 8]
                first += [r * m, r * md, r * mc, s * dd, s * dc]
                second += [no_terms, r * dc, r * cc]
            a_high, a_low = split(jnp.concatenate(first + [no_tail], axis=0))
            b_high, b_low = split(jnp.concatenate(second + [no_tail], axis=0))
            left = jnp.concatenate([c_high, c_low, c_high, d_high, d_low, d_high], axis=1)
            a_high, a_low, b_high, b_low = a_high.T, a_low.T, b_high.T, b_low.T
            right = jnp.concatenate([a_high, a_high, a_low, b_high, b_high, b_low], axis=0)
            sums = jnp.dot(left, right, preferred_element_type=F32)
            for v in range(SPAN // 8):
                spread[k, PAD // 8 + v] = sums[8 * v : 8 * v + 8]
        held = [spread[k, pl.ds(bases[k], COLS // 8)] for k in range(8)]
        for v in range(COLS // 8):
            total = grid[step, 8 * v : 8 * v + 8, :]
            for part in held:
                total = total + part[v]
            grid[step, 8 * v : 8 * v + 8, :] = total

    def gather(step, batch, source, order, target, pitch):
        parts = [[] for _ in range(6)]
        for k in range(8):
            position = batch * 8 + k
            slot = tables[order, position]
            block = slot if step == 0 else tables[SOURCE_1, position]
            group = lax.shift_right_logical(anchor_cross[step, slot] + GHOST, 4)
            cols = cols_kept[block]
            moved = lax.dot_general(
                window[group],
                jnp.concatenate([cols, cols], axis=0),
                (((1,), (0,)), ((), ())),
                preferred_element_type=F32,
            )
            rows = rows_kept[block]
            sums = [None] * 6
            for g in range(3):
                r, s = rows[8 * g : 8 * g + 8], rows[24 + 8 * g : 32 + 8 * g]
                down, cross = moved[16 * g : 16 * g + 8], moved[16 * g + 8 : 16 * g + 16]
                terms = [
                    r * down[:, :LANES],
                    r * cross[:, :LANES],
                    s * down[:, :LANES],
                    s * cross[:, :LANES],
                    r * down[:, LANES:],
                    r * cross[:, LANES:],
                ]
                sums = [t if a is None else a + t for a, t in zip(sums, terms)]
            for held, total in zip(parts, sums):
                held.append(total)
            stage[PITCH * k : PITCH * k + PITCH, :] = source[block]
        new_down, new_cross, l_dd, l_cd, l_dc, l_cc = (sum_rows(p, sublane) for p in parts)
        f = strided(stage, 0, PITCH)
        rate_dc = 0.5 * (l_dc + l_cd)
        trace = l_dd + l_cc
        shear, lame = f[9], f[10]
        updated = [
            jnp.clip(f[0] + TIME_STEP * new_down, 0.5, WIN_DOWN - 1.5),
            jnp.clip(f[1] + TIME_STEP * new_cross, 0.5, WIN_CROSS - 1.5),
            new_down,
            new_cross,
            f[4] + TIME_STEP * (lame * trace + 2.0 * shear * l_dd),
            f[5] + TIME_STEP * (2.0 * shear * rate_dc),
            f[6] + TIME_STEP * (lame * trace + 2.0 * shear * l_cc),
            f[7],
            f[8] * (1.0 + TIME_STEP * trace),
            shear,
            lame,
            f[11] + TIME_STEP * (l_dd * l_dd + l_cc * l_cc + 2.0 * rate_dc * rate_dc),
        ]
        put_strided(target, batch * 8 * pitch, pitch, updated)

    def remote(source, target, send, recv, step):
        return pltpu.make_async_remote_copy(
            src_ref=source,
            dst_ref=target,
            send_sem=send,
            recv_sem=recv,
            device_id=at(step),
            device_id_type=MESH,
        )

    def exchange(step):
        first = grid.at[step, pl.ds(0, 8), :]
        last = grid.at[step, pl.ds(TILE_CROSS, 8), :]
        messages = [
            ((0, 1), last, col_in.at[step, 0]),
            ((0, -1), first, col_in.at[step, 1]),
            ((1, 1), last, col_in.at[step, 2]),
            ((-1, 1), last, col_in.at[step, 3]),
            ((1, -1), first, col_in.at[step, 4]),
            ((-1, -1), first, col_in.at[step, 5]),
            ((1, 0), last, col_in.at[step, 6]),
            ((-1, 0), last, col_in.at[step, 7]),
            ((1, 0), turned.at[step, pl.ds(2 * BAND, BAND), :], band_in.at[step, 0]),
            ((-1, 0), turned.at[step, pl.ds(0, BAND), :], band_in.at[step, 1]),
        ]
        copies = [
            remote(source, target, halo_send.at[step, n], halo_recv.at[step, n], near)
            for n, (near, source, target) in enumerate(messages)
        ]
        for copy in copies[:8]:
            copy.start()
        for t in range(2):
            side = slice(LANES * t, LANES * (t + 1))
            turned[step, :, side] = grid[step, side, :].T[: 3 * BAND]
        for copy in copies[8:]:
            copy.start()
        return copies

    def velocities(step):
        above = me_down > 0
        below = me_down < size_down - 1
        before = me_cross > 0
        after = me_cross < size_cross - 1
        low = lane8 < BAND
        high = (lane8 >= 2 * BAND) & (lane8 < 3 * BAND)
        few = lane8 < 8

        def from_above(there, n):
            return jnp.where(low & above & there, pltpu.roll(col_in[step, n], 48, 1), 0.0)

        def from_below(there, n):
            return jnp.where(high & below & there, pltpu.roll(col_in[step, n], 80, 1), 0.0)

        first = jnp.where(before, col_in[step, 0], 0.0) + from_above(before, 2) + from_below(before, 3)
        last = grid[step, TILE_CROSS : TILE_CROSS + 8, :] + jnp.where(after, col_in[step, 1], 0.0)
        last = last + from_above(after, 4) + from_below(after, 5)
        last = last + from_above(True, 6) + from_below(True, 7)
        edge = jnp.concatenate([first, last, jnp.zeros((LANES - 16, LANES), F32)], axis=0).T

        tiles = []
        for t in range(3):
            col_global = me_cross * TILE_CROSS - GHOST + LANES * t + lane8
            col_keep = (col_global > 0) & (col_global < TILE_CROSS * size_cross - 1)
            side = slice(LANES * t, LANES * (t + 1))
            found = []
            for g in range(3):
                row_global = me_down * TILE_DOWN - GHOST + 8 * g + sublane
                inside = col_keep & (row_global > 0) & (row_global < TILE_DOWN * size_down - 1)
                sums = []
                for channel in range(5):
                    here = slice(BAND * g + 8 * channel, BAND * g + 8 * channel + 8)
                    if t == 2:
                        sums.append(jnp.where(few, pltpu.roll(edge[here], LANES - 8, 1), 0.0))
                        continue
                    total = turned[step, here, side]
                    there = slice(8 * channel, 8 * channel + 8)
                    if g == 0:
                        total = total + jnp.where(above, band_in[step, 0, there, side], 0.0)
                    if g == 2:
                        total = total + jnp.where(below, band_in[step, 1, there, side], 0.0)
                    if t == 0:
                        total = total + jnp.where(few, edge[here], 0.0)
                    sums.append(total)
                mass, moved_down, moved_cross, force_down, force_cross = sums
                heavy = jnp.maximum(mass, MASS_FLOOR)
                v_down = (moved_down + TIME_STEP * (force_down + GRAVITY * mass)) / heavy
                v_cross = (moved_cross + TIME_STEP * force_cross) / heavy
                found += [jnp.where(inside, v_down, 0.0), jnp.where(inside, v_cross, 0.0)]
            tiles.append(jnp.concatenate(found, axis=0))
        tops = [x.astype(BF16).astype(F32) for x in tiles]
        rests = [x - top for x, top in zip(tiles, tops)]
        lane48 = lax.broadcasted_iota(jnp.int32, (48, LANES), 1)

        def turn(x, m):
            return pltpu.roll(x, 16 * m, 1) if m else x

        def side_by_side(a, b, c, d):
            return jnp.where(
                lane48 < 64,
                jnp.where(lane48 < 32, a, b),
                jnp.where(lane48 < 96, c, d),
            ).astype(BF16)

        for t in range(2):
            high_turned = [turn(tops[t], m) for m in range(8)]
            low_turned = [turn(rests[t], m) for m in range(8)]
            for q in range(7):
                window[8 * t + q] = side_by_side(
                    high_turned[(8 - q) % 8],
                    high_turned[(10 - q) % 8],
                    low_turned[(12 - q) % 8],
                    low_turned[(14 - q) % 8],
                )
            a = jnp.where(lane48 < 16, tops[t + 1], tops[t])
            b = jnp.where(lane48 < 16, rests[t + 1], rests[t])
            window[8 * t + 7] = side_by_side(turn(a, 1), turn(a, 3), turn(b, 5), turn(b, 7))

    def wait_all(copies):
        for copy in copies:
            copy.wait()

    def send_blocks(step):
        copies = []
        for k, near in enumerate(MOVES):
            copy = remote(
                leaving.at[step, pl.ds(k * SLOTS * FIELDS, SEND_ROWS), :],
                arrived.at[step, pl.ds((k ^ 1) * SLOTS * FIELDS, SEND_ROWS), :],
                move_send.at[step, k],
                move_recv.at[step, k],
                near,
            )
            copy.start()
            copies.append(copy)
        return copies

    for step in range(STEPS):
        grid[step] = jnp.zeros((COLS, LANES), F32)

    def scatter_0(batch, carry):
        rows = pl.ds(pl.multiple_of(batch * 8, 8), 8)
        fields = [fields_in[i, rows, :] for i in range(FIELDS)]
        put_strided(flat_0, batch * 8 * PITCH, PITCH, fields)
        scatter(0, batch, fields)
        return carry

    batches = BLOCKS // 8
    for n, load in enumerate(loads):
        load.wait()
        lax.fori_loop(n * batches // LOADS, (n + 1) * batches // LOADS, scatter_0, 0)
    pl.semaphore_wait(barrier, len(NEAR))
    wait_all(exchange(0))
    velocities(0)

    def gather_leaving_0(batch, carry):
        gather(0, batch, state_0, ORDER_0, leaving.at[0], FIELDS)
        return carry

    def gather_staying_0(batch, carry):
        gather(0, batch, state_0, ORDER_0, flat_1, PITCH)
        return carry

    lax.fori_loop(0, 8, gather_leaving_0, 0)
    copies = send_blocks(0)
    lax.fori_loop(8, 16, gather_staying_0, 0)

    def settled(step, batch):
        here = (lax.rem(batch, 2) * 8 + sublane) < count[step, batch // 2]
        first = batch * 8 * FIELDS
        came = strided(arrived.at[step], first, FIELDS)
        kept = strided(leaving.at[step], first, FIELDS)
        return [jnp.where(here, a, b) for a, b in zip(came, kept)]

    def scatter_staying(batch, carry):
        scatter(1, batch, strided(flat_1, batch * 8 * PITCH, PITCH))
        return carry

    def scatter_arrived(batch, carry):
        fields = settled(0, batch)
        put_strided(flat_1, batch * 8 * PITCH, PITCH, fields)
        scatter(1, batch, fields)
        return carry

    lax.fori_loop(8, 16, scatter_staying, 0)
    wait_all(copies)
    lax.fori_loop(0, 8, scatter_arrived, 0)
    wait_all(exchange(1))
    velocities(1)

    def gather_leaving_1(batch, carry):
        gather(1, batch, state_1, ORDER_1, leaving.at[1], FIELDS)
        return carry

    def gather_staying_1(batch, carry):
        gather(1, batch, state_1, ORDER_1, flat_2, PITCH)
        return carry

    lax.fori_loop(0, 8, gather_leaving_1, 0)
    copies = send_blocks(1)
    lax.fori_loop(8, 16, gather_staying_1, 0)
    wait_all(copies)

    def settle(batch, carry):
        put_strided(flat_2, batch * 8 * PITCH, PITCH, settled(1, batch))
        return carry

    lax.fori_loop(0, 8, settle, 0)

    def put(batch, carry):
        for k in range(8):
            place = tables[PLACE_1, batch * 8 + k]
            stage[PITCH * k : PITCH * k + PITCH, :] = state_2[place]
        rows = pl.ds(pl.multiple_of(batch * 8, 8), 8)
        for i, x in enumerate(strided(stage, 0, PITCH)):
            result[i, rows, :] = x
        return carry

    lax.fori_loop(0, BLOCKS // 8, put, 0)


def slot_tables(move_slots):
    listed = move_slots.reshape(STEPS, 4 * MOVE_CAP, 1)
    slot = jnp.arange(BLOCKS, dtype=jnp.int32)
    same = listed == slot
    number = jnp.arange(4 * MOVE_CAP, dtype=jnp.int32)[:, None]
    position = number + (SLOTS - MOVE_CAP) * (number // MOVE_CAP)
    used = jnp.sum(same.astype(jnp.int32), axis=1)
    there = jnp.sum(jnp.where(same, position, 0), axis=1)
    earlier = jnp.sum((listed < slot).astype(jnp.int32), axis=1)
    rank = slot - earlier
    spare = 4 * (SLOTS - MOVE_CAP)
    third = rank // (SLOTS - MOVE_CAP)
    free = jnp.where(
        rank < spare,
        SLOTS * third + MOVE_CAP + rank - (SLOTS - MOVE_CAP) * third,
        4 * MOVE_CAP + rank,
    )
    place = jnp.where(used > 0, there, free)
    held = place[:, None, :] == slot[None, :, None]
    order = jnp.sum(jnp.where(held, slot, 0), axis=2)
    source = jnp.sum(jnp.where(held[1], place[0], 0), axis=1)
    return jnp.stack([order[0], order[1], source, place[1]])


def on_device(particles, anchor_down, anchor_cross, move_count, move_slots):
    smem = pl.BlockSpec(memory_space=pltpu.SMEM)
    vmem = pl.BlockSpec(memory_space=pltpu.VMEM)
    by_field = pl.pallas_call(
        kernel,
        out_shape=jax.ShapeDtypeStruct((FIELDS, BLOCKS, LANES), F32),
        in_specs=[smem, smem, smem, smem, pl.BlockSpec(memory_space=pltpu.HBM)],
        out_specs=vmem,
        scratch_shapes=[
            pltpu.VMEM((FIELDS, BLOCKS, LANES), F32),
            pltpu.VMEM((8 * PITCH + STRIDE_PAD, LANES), F32),
            pltpu.VMEM((BLOCKS, 48, LANES), F32),
            pltpu.VMEM((BLOCKS, 2 * SPAN, 2 * LANES), BF16),
            pltpu.VMEM((8, (PAD + SPAN + PAD) // 8, 8, LANES), F32),
            pltpu.VMEM((STEPS, COLS, LANES), F32),
            pltpu.VMEM((STEPS, 3 * BAND, 2 * LANES), F32),
            pltpu.VMEM((STEPS, 2, BAND, 2 * LANES), F32),
            pltpu.VMEM((STEPS, 8, 8, LANES), F32),
            pltpu.VMEM((16, 48, LANES), BF16),
            pltpu.VMEM((STEPS, OUT_ROWS + STRIDE_PAD, LANES), F32),
            pltpu.VMEM((STEPS, OUT_ROWS + STRIDE_PAD, LANES), F32),
            pltpu.VMEM((BLOCKS + 1, PITCH, LANES), F32),
            pltpu.VMEM((BLOCKS + 1, PITCH, LANES), F32),
            pltpu.VMEM((BLOCKS + 1, PITCH, LANES), F32),
            pltpu.SemaphoreType.DMA((STEPS, 10)),
            pltpu.SemaphoreType.DMA((STEPS, 10)),
            pltpu.SemaphoreType.DMA((STEPS, 4)),
            pltpu.SemaphoreType.DMA((STEPS, 4)),
            pltpu.SemaphoreType.DMA((LOADS,)),
        ],
        compiler_params=pltpu.CompilerParams(
            collective_id=0, has_side_effects=True, vmem_limit_bytes=40 * 1024 * 1024
        ),
    )(
        slot_tables(move_slots),
        anchor_down,
        anchor_cross,
        move_count[:, :, 0, 0],
        jnp.transpose(particles, (1, 0, 2)),
    )
    return jnp.transpose(by_field, (1, 0, 2))


def solution(mesh):
    return jax.shard_map(
        on_device,
        mesh=mesh,
        in_specs=(
            P(("down", "cross"), None, None),
            P(None, ("down", "cross")),
            P(None, ("down", "cross")),
            P(None, None, "down", "cross"),
            P(None, None, None, "down", "cross"),
        ),
        out_specs=P(("down", "cross"), None, None),
        check_vma=False,
    )
```

time: 65.3 us -> 53.9 us (0.83)
  Pallas kernels: 61 us -> 48.8 us
  other arithmetic: 0.39 us -> 1.12 us
    pallas_call x1, Pallas kernels: 61 us -> 48.8 us  [on_device(): pl.pallas_call(kernel, out_shape=jax.ShapeDtypeStruct((FIELDS, BLOCKS, LA...]
    unnamed x7 -> x12, local copies, waits for them, and re-layouts: 1.64 us -> 3.37 us
    pallas_call x1 -> x0, local copies, waits for them, and re-layouts: 1.12 us -> none  [on_device(): pl.pallas_call(kernel, out_shape=jax.ShapeDtypeStruct(particles.shape, F3...]
    pad x1 -> x0, local copies, waits for them, and re-layouts: 0.69 us -> none  [slot_tables(): jnp.pad(move_slots[:, :, :, 0, 0], ((0, 0), (0, 0), (0, SLOTS - MOVE_CAP)...]
    unnamed x0 -> x1, other arithmetic: none -> 0.67 us
where the time goes in v2:
time: 53.9 us; the launch traced here: 53.6 us
  Pallas kernels  48.8 us (91%)
  local copies, waits for them, and re-layouts  3.56 us (7%)
  other arithmetic  1.12 us (2%)
    pallas_call x1, Pallas kernels, on_device(): pl.pallas_call(kernel, out_shape=jax.ShapeDtypeStruct((FIELDS, BLOCKS, LA...  48.8 us
    unnamed x12, local copies, waits for them, and re-layouts  3.37 us

profile of v2, /device:TPU:6, one launch (start us, length us, event | category | flops | bytes accessed | tf_op | source)
XLA Modules:
  0.0 53.6 jit_solution(9324609507053366506)
XLA Ops:
  0.0 0.0 copy-start.4
  0.0 0.5 broadcast.72
  0.5 0.2 copy-done.4
  0.7 0.7 %reduce.3 = s32[2,4,13]{2,1,0:T(4,128)S(1)} reduce(s32[2,4,13,1,1]{2,4,3,1,0:T(1,128)S(1)} %copy-done.4, s32[]{:T(128)} %broadcast.72), dimensions={3,4}, to_apply=%param.9.reduce_sub_computation.3 | reduce | bytes 836 | tf_op args[4]
  1.4 0.1 eq.30
  1.4 0.1 copy.6
  1.5 0.2 fusion
  1.8 0.1 select_reduce_fusion
  1.9 0.1 select_reduce_fusion.1
  2.0 0.0 copy-start.1
  2.0 0.0 copy-start.2
  2.0 0.0 copy-start.3
  2.1 0.6 %copy-done.1 = s32[2,128]{1,0:T(2,128)S(1)} copy-done((s32[2,128]{1,0:T(2,128)S(1)}, s32[2,128]{1,0:T(2,128)}, u32[]{:S(2)}) %copy-start.1) | copy-done | bytes 1048
  2.7 0.0 copy-done.2
  2.7 0.0 copy-done.3
  2.7 0.0 copy-start
  2.7 1.1 %copy-done = f32[128,12,128]{2,0,1:T(8,128)S(1)} copy-done((f32[128,12,128]{2,0,1:T(8,128)S(1)}, f32[128,12,128]{2,0,1:T(8,128)}, u32[]{:S(2)}) %copy-start) | copy-done | bytes 786456
  3.9 48.8 %shard_map.55 = f32[12,128,128]{2,1,0:T(8,128)S(1)} custom-call(s32[4,128]{1,0:T(4,128)S(1)} %pad_add_fusion.tables, s32[2,128]{1,0:T(2,128)S(1)} %copy-done.1, s32[2,128]{1,0:T(2,128)S(1)} %copy-done.2, s32[2,4]{1,0:T(2,128)S(1)} %bitcast.13, f32[12,128,128]{2,1,0:T(8,128)S(1)} %bitcast.12), custom_call_target="tpu_custom_call" | custom-call | tf_op jit(solution)/shard_map/pallas_call | solution.py:494
  52.7 0.9 %copy.8 = f32[128,12,128]{2,0,1:T(8,128)} copy(f32[128,12,128]{2,0,1:T(8,128)S(1)} %bitcast.11) | data formatting | bytes 1572864
  (5 shorter events, 0.1 us)
Async XLA Ops:
  0.0 0.7 %copy-start.4 = (s32[2,4,13,1,1]{2,4,3,1,0:T(1,128)S(1)}, s32[2,4,13,1,1]{2,4,3,1,0:T(1,128)}, u32[]{:S(2)}) copy-start(s32[2,4,13,1,1]{2,4,3,1,0:T(1,128)} %param.9) | copy-start | bytes 1252
  2.0 0.7 %copy-start.1 = (s32[2,128]{1,0:T(2,128)S(1)}, s32[2,128]{1,0:T(2,128)}, u32[]{:S(2)}) copy-start(s32[2,128]{1,0:T(2,128)} %anchor_down.1) | copy-start | bytes 3076
  2.0 0.7 %copy-start.2 = (s32[2,128]{1,0:T(2,128)S(1)}, s32[2,128]{1,0:T(2,128)}, u32[]{:S(2)}) copy-start(s32[2,128]{1,0:T(2,128)} %anchor_cross.1) | copy-start | bytes 3076
  2.0 0.7 %copy-start.3 = (s32[2,4,1,1]{1,3,2,0:T(1,128)S(1)}, s32[2,4,1,1]{1,3,2,0:T(1,128)}, u32[]{:S(2)}) copy-start(s32[2,4,1,1]{1,3,2,0:T(1,128)} %param.8) | copy-start | bytes 100
  2.7 1.1 %copy-start = (f32[128,12,128]{2,0,1:T(8,128)S(1)}, f32[128,12,128]{2,0,1:T(8,128)}, u32[]{:S(2)}) copy-start(f32[128,12,128]{2,0,1:T(8,128)} %param.5) | copy-start | bytes 2359300

commit v3 on v2

--- a/solution.py
+++ b/solution.py
@@ -33,6 +33,8 @@
 ALL_ROWS = BLOCKS * PITCH
 SEND_ROWS = 8 * -(-MOVE_CAP * FIELDS // 8)
 STRIDE_PAD = 16
+SCATTER_BATCHES = 4
+GATHER_BATCHES = 4
 LOADS = 4
 ORDER_0, ORDER_1, SOURCE_1, PLACE_1 = range(4)
 
@@ -138,7 +140,7 @@
     no_terms = jnp.zeros((BAND - 16, LANES), F32)
     no_tail = jnp.zeros((8, LANES), F32)
 
-    for k in range(8):
+    for k in range(8 * SCATTER_BATCHES):
         spread[k] = jnp.zeros(((PAD + SPAN + PAD) // 8, 8, LANES), F32)
 
     def strided(ref, first, pitch):
@@ -151,11 +153,10 @@
     def slot_of(step, block):
         return block if step == 0 else tables[ORDER_0, block]
 
-    def scatter(step, batch, fields):
+    def scatter_one(step, batch, fields, at_spread, bases):
         u, w, v_down, v_cross, s_dd, s_dc, s_cc, mass, volume = fields[:9]
         less = -volume
         values = [mass, mass * v_down, mass * v_cross, less * s_dd, less * s_dc, less * s_cc]
-        bases = []
         for k in range(8):
             block = batch * 8 + k
             slot = slot_of(step, block)
@@ -185,15 +186,21 @@
             right = jnp.concatenate([a_high, a_high, a_low, b_high, b_high, b_low], axis=0)
             sums = jnp.dot(left, right, preferred_element_type=F32)
             for v in range(SPAN // 8):
-                spread[k, PAD // 8 + v] = sums[8 * v : 8 * v + 8]
-        held = [spread[k, pl.ds(bases[k], COLS // 8)] for k in range(8)]
+                spread[at_spread + k, PAD // 8 + v] = sums[8 * v : 8 * v + 8]
+
+    def scatter(step, group, fields_of):
+        bases = []
+        for n in range(SCATTER_BATCHES):
+            batch = group * SCATTER_BATCHES + n
+            scatter_one(step, batch, fields_of(batch), 8 * n, bases)
+        held = [spread[k, pl.ds(base, COLS // 8)] for k, base in enumerate(bases)]
         for v in range(COLS // 8):
             total = grid[step, 8 * v : 8 * v + 8, :]
             for part in held:
                 total = total + part[v]
             grid[step, 8 * v : 8 * v + 8, :] = total
 
-    def gather(step, batch, source, order, target, pitch):
+    def gather_one(step, batch, source, order, target, pitch, at_stage):
         parts = [[] for _ in range(6)]
         for k in range(8):
             position = batch * 8 + k
@@ -223,9 +230,9 @@
                 sums = [t if a is None else a + t for a, t in zip(sums, terms)]
             for held, total in zip(parts, sums):
                 held.append(total)
-            stage[PITCH * k : PITCH * k + PITCH, :] = source[block]
+            stage[at_stage + PITCH * k : at_stage + PITCH * k + PITCH, :] = source[block]
         new_down, new_cross, l_dd, l_cd, l_dc, l_cc = (sum_rows(p, sublane) for p in parts)
-        f = strided(stage, 0, PITCH)
+        f = strided(stage, at_stage, PITCH)
         rate_dc = 0.5 * (l_dc + l_cd)
         trace = l_dd + l_cc
         shear, lame = f[9], f[10]
@@ -245,6 +252,11 @@
         ]
         put_strided(target, batch * 8 * pitch, pitch, updated)
 
+    def gather(step, group, source, order, target, pitch):
+        for n in range(GATHER_BATCHES):
+            batch = group * GATHER_BATCHES + n
+            gather_one(step, batch, source, order, target, pitch, 8 * PITCH * n)
+
     def remote(source, target, send, recv, step):
         return pltpu.make_async_remote_copy(
             src_ref=source,
@@ -259,14 +271,14 @@
         first = grid.at[step, pl.ds(0, 8), :]
         last = grid.at[step, pl.ds(TILE_CROSS, 8), :]
         messages = [
-            ((0, 1), last, col_in.at[step, 0]),
-            ((0, -1), first, col_in.at[step, 1]),
             ((1, 1), last, col_in.at[step, 2]),
             ((-1, 1), last, col_in.at[step, 3]),
             ((1, -1), first, col_in.at[step, 4]),
             ((-1, -1), first, col_in.at[step, 5]),
             ((1, 0), last, col_in.at[step, 6]),
             ((-1, 0), last, col_in.at[step, 7]),
+            ((0, 1), last, col_in.at[step, 0]),
+            ((0, -1), first, col_in.at[step, 1]),
             ((1, 0), turned.at[step, pl.ds(2 * BAND, BAND), :], band_in.at[step, 0]),
             ((-1, 0), turned.at[step, pl.ds(0, BAND), :], band_in.at[step, 1]),
         ]
@@ -366,9 +378,10 @@
         for copy in copies:
             copy.wait()
 
-    def send_blocks(step):
+    def send_blocks(step, first):
         copies = []
-        for k, near in enumerate(MOVES):
+        for k in (first, first + 1):
+            near = MOVES[k]
             copy = remote(
                 leaving.at[step, pl.ds(k * SLOTS * FIELDS, SEND_ROWS), :],
                 arrived.at[step, pl.ds((k ^ 1) * SLOTS * FIELDS, SEND_ROWS), :],
@@ -383,14 +396,17 @@
     for step in range(STEPS):
         grid[step] = jnp.zeros((COLS, LANES), F32)
 
-    def scatter_0(batch, carry):
+    def fields_0(batch):
         rows = pl.ds(pl.multiple_of(batch * 8, 8), 8)
         fields = [fields_in[i, rows, :] for i in range(FIELDS)]
         put_strided(flat_0, batch * 8 * PITCH, PITCH, fields)
-        scatter(0, batch, fields)
-        return carry
-
-    batches = BLOCKS // 8
+        return fields
+
+    def scatter_0(group, carry):
+        scatter(0, group, fields_0)
+        return carry
+
+    batches = BLOCKS // 8 // SCATTER_BATCHES
     for n, load in enumerate(loads):
         load.wait()
         lax.fori_loop(n * batches // LOADS, (n + 1) * batches // LOADS, scatter_0, 0)
@@ -406,9 +422,11 @@
         gather(0, batch, state_0, ORDER_0, flat_1, PITCH)
         return carry
 
-    lax.fori_loop(0, 8, gather_leaving_0, 0)
-    copies = send_blocks(0)
-    lax.fori_loop(8, 16, gather_staying_0, 0)
+    lax.fori_loop(0, 1, gather_leaving_0, 0)
+    copies = send_blocks(0, 0)
+    lax.fori_loop(1, 2, gather_leaving_0, 0)
+    copies += send_blocks(0, 2)
+    lax.fori_loop(2, 4, gather_staying_0, 0)
 
     def settled(step, batch):
         here = (lax.rem(batch, 2) * 8 + sublane) < count[step, batch // 2]
@@ -417,19 +435,25 @@
         kept = strided(leaving.at[step], first, FIELDS)
         return [jnp.where(here, a, b) for a, b in zip(came, kept)]
 
-    def scatter_staying(batch, carry):
-        scatter(1, batch, strided(flat_1, batch * 8 * PITCH, PITCH))
-        return carry
-
-    def scatter_arrived(batch, carry):
+    def fields_staying(batch):
+        return strided(flat_1, batch * 8 * PITCH, PITCH)
+
+    def fields_arrived(batch):
         fields = settled(0, batch)
         put_strided(flat_1, batch * 8 * PITCH, PITCH, fields)
-        scatter(1, batch, fields)
-        return carry
-
-    lax.fori_loop(8, 16, scatter_staying, 0)
+        return fields
+
+    def scatter_staying(group, carry):
+        scatter(1, group, fields_staying)
+        return carry
+
+    def scatter_arrived(group, carry):
+        scatter(1, group, fields_arrived)
+        return carry
+
+    lax.fori_loop(2, 4, scatter_staying, 0)
     wait_all(copies)
-    lax.fori_loop(0, 8, scatter_arrived, 0)
+    lax.fori_loop(0, 2, scatter_arrived, 0)
     wait_all(exchange(1))
     velocities(1)
 
@@ -441,9 +465,11 @@
         gather(1, batch, state_1, ORDER_1, flat_2, PITCH)
         return carry
 
-    lax.fori_loop(0, 8, gather_leaving_1, 0)
-    copies = send_blocks(1)
-    lax.fori_loop(8, 16, gather_staying_1, 0)
+    lax.fori_loop(0, 1, gather_leaving_1, 0)
+    copies = send_blocks(1, 0)
+    lax.fori_loop(1, 2, gather_leaving_1, 0)
+    copies += send_blocks(1, 2)
+    lax.fori_loop(2, 4, gather_staying_1, 0)
     wait_all(copies)
 
     def settle(batch, carry):
@@ -498,10 +524,10 @@
         out_specs=vmem,
         scratch_shapes=[
             pltpu.VMEM((FIELDS, BLOCKS, LANES), F32),
-            pltpu.VMEM((8 * PITCH + STRIDE_PAD, LANES), F32),
+            pltpu.VMEM((8 * PITCH * GATHER_BATCHES + STRIDE_PAD, LANES), F32),
             pltpu.VMEM((BLOCKS, 48, LANES), F32),
             pltpu.VMEM((BLOCKS, 2 * SPAN, 2 * LANES), BF16),
-            pltpu.VMEM((8, (PAD + SPAN + PAD) // 8, 8, LANES), F32),
+            pltpu.VMEM((8 * SCATTER_BATCHES, (PAD + SPAN + PAD) // 8, 8, LANES), F32),
             pltpu.VMEM((STEPS, COLS, LANES), F32),
             pltpu.VMEM((STEPS, 3 * BAND, 2 * LANES), F32),
             pltpu.VMEM((STEPS, 2, BAND, 2 * LANES), F32),

time: 53.9 us -> 47.7 us (0.88)
  Pallas kernels: 48.8 us -> 42.8 us
    pallas_call x1, Pallas kernels: 48.8 us -> 42.8 us  [on_device(): pl.pallas_call(kernel, out_shape=jax.ShapeDtypeStruct((FIELDS, BLOCKS, LA...]
where the time goes in v3:
time: 47.7 us; the launch traced here: 47.6 us
  Pallas kernels  42.8 us (90%)
  local copies, waits for them, and re-layouts  3.56 us (7%)
  other arithmetic  1.12 us (2%)
    pallas_call x1, Pallas kernels, on_device(): pl.pallas_call(kernel, out_shape=jax.ShapeDtypeStruct((FIELDS, BLOCKS, LA...  42.8 us
    unnamed x12, local copies, waits for them, and re-layouts  3.37 us

profile of v3, /device:TPU:6, one launch (start us, length us, event | category | flops | bytes accessed | tf_op | source)
XLA Modules:
  0.0 47.6 jit_solution(4158358166858435005)
XLA Ops:
  0.0 0.0 copy-start.4
  0.0 0.5 %broadcast.72 = s32[]{:T(128)} broadcast(s32[]{:T(128)} %constant.51), dimensions={} | broadcast | bytes 8 | tf_op args[4]
  0.5 0.2 copy-done.4
  0.7 0.7 %reduce.3 = s32[2,4,13]{2,1,0:T(4,128)S(1)} reduce(s32[2,4,13,1,1]{2,4,3,1,0:T(1,128)S(1)} %copy-done.4, s32[]{:T(128)} %broadcast.72), dimensions={3,4}, to_apply=%param.9.reduce_sub_computation.3 | reduce | bytes 836 | tf_op args[4]
  1.4 0.1 eq.30
  1.4 0.1 copy.6
  1.5 0.2 fusion
  1.8 0.1 select_reduce_fusion
  1.9 0.1 select_reduce_fusion.1
  2.0 0.0 copy-start.1
  2.0 0.0 copy-start.2
  2.0 0.0 copy-start.3
  2.1 0.6 %copy-done.1 = s32[2,128]{1,0:T(2,128)S(1)} copy-done((s32[2,128]{1,0:T(2,128)S(1)}, s32[2,128]{1,0:T(2,128)}, u32[]{:S(2)}) %copy-start.1) | copy-done | bytes 1048
  2.7 0.0 copy-done.2
  2.7 0.0 copy-done.3
  2.7 0.0 copy-start
  2.7 1.1 %copy-done = f32[128,12,128]{2,0,1:T(8,128)S(1)} copy-done((f32[128,12,128]{2,0,1:T(8,128)S(1)}, f32[128,12,128]{2,0,1:T(8,128)}, u32[]{:S(2)}) %copy-start) | copy-done | bytes 786456
  3.9 42.8 %shard_map.55 = f32[12,128,128]{2,1,0:T(8,128)S(1)} custom-call(s32[4,128]{1,0:T(4,128)S(1)} %pad_add_fusion.tables, s32[2,128]{1,0:T(2,128)S(1)} %copy-done.1, s32[2,128]{1,0:T(2,128)S(1)} %copy-done.2, s32[2,4]{1,0:T(2,128)S(1)} %bitcast.13, f32[12,128,128]{2,1,0:T(8,128)S(1)} %bitcast.12), custom_call_target="tpu_custom_call" | custom-call | tf_op jit(solution)/shard_map/pallas_call | solution.py:520
  46.7 0.9 %copy.8 = f32[128,12,128]{2,0,1:T(8,128)} copy(f32[128,12,128]{2,0,1:T(8,128)S(1)} %bitcast.11) | data formatting | bytes 1572864
  (5 shorter events, 0.1 us)
Async XLA Ops:
  0.0 0.7 %copy-start.4 = (s32[2,4,13,1,1]{2,4,3,1,0:T(1,128)S(1)}, s32[2,4,13,1,1]{2,4,3,1,0:T(1,128)}, u32[]{:S(2)}) copy-start(s32[2,4,13,1,1]{2,4,3,1,0:T(1,128)} %param.9) | copy-start | bytes 1252
  2.0 0.7 %copy-start.1 = (s32[2,128]{1,0:T(2,128)S(1)}, s32[2,128]{1,0:T(2,128)}, u32[]{:S(2)}) copy-start(s32[2,128]{1,0:T(2,128)} %anchor_down.1) | copy-start | bytes 3076
  2.0 0.7 %copy-start.2 = (s32[2,128]{1,0:T(2,128)S(1)}, s32[2,128]{1,0:T(2,128)}, u32[]{:S(2)}) copy-start(s32[2,128]{1,0:T(2,128)} %anchor_cross.1) | copy-start | bytes 3076
  2.0 0.7 %copy-start.3 = (s32[2,4,1,1]{1,3,2,0:T(1,128)S(1)}, s32[2,4,1,1]{1,3,2,0:T(1,128)}, u32[]{:S(2)}) copy-start(s32[2,4,1,1]{1,3,2,0:T(1,128)} %param.8) | copy-start | bytes 100
  2.7 1.1 %copy-start = (f32[128,12,128]{2,0,1:T(8,128)S(1)}, f32[128,12,128]{2,0,1:T(8,128)}, u32[]{:S(2)}) copy-start(f32[128,12,128]{2,0,1:T(8,128)} %param.5) | copy-start | bytes 2359300

commit v4 on v3

--- a/solution.py
+++ b/solution.py
@@ -80,10 +80,10 @@
 
 
 def kernel(
-    tables,
-    anchor_down,
-    anchor_cross,
-    count,
+    move_slots_hbm,
+    anchor_down_hbm,
+    anchor_cross_hbm,
+    count_hbm,
     fields_hbm,
     result,
     fields_in,
@@ -106,6 +106,14 @@
     move_send,
     move_recv,
     load_sem,
+    tables_made,
+    tables,
+    table_sem,
+    move_slots,
+    anchor_down,
+    anchor_cross,
+    count,
+    small_sem,
 ):
     flat_0 = state_0.reshape(ALL_ROWS + STRIDE_PAD, LANES)
     flat_1 = state_1.reshape(ALL_ROWS + STRIDE_PAD, LANES)
@@ -119,6 +127,19 @@
             lax.rem(me_cross + step[1] + size_cross, size_cross),
         )
 
+    small = [
+        pltpu.make_async_copy(source, target, small_sem.at[n])
+        for n, (source, target) in enumerate(
+            (
+                (move_slots_hbm, move_slots),
+                (anchor_down_hbm, anchor_down),
+                (anchor_cross_hbm, anchor_cross),
+                (count_hbm, count),
+            )
+        )
+    ]
+    for copy in small:
+        copy.start()
     loads = []
     for n in range(LOADS):
         part = pl.ds(n * BLOCKS // LOADS, BLOCKS // LOADS)
@@ -142,6 +163,40 @@
 
     for k in range(8 * SCATTER_BATCHES):
         spread[k] = jnp.zeros(((PAD + SPAN + PAD) // 8, 8, LANES), F32)
+
+    for copy in small:
+        copy.wait()
+    slot = lax.broadcasted_iota(jnp.int32, (1, LANES), 1)
+    spare = SLOTS - MOVE_CAP
+    places, held = [], []
+    for step in range(STEPS):
+        place = jnp.full((1, LANES), -1, jnp.int32)
+        rank = slot
+        for n in range(4 * MOVE_CAP):
+            k, m = divmod(n, MOVE_CAP)
+            listed = move_slots[4 * step + k, 0, m]
+            place = jnp.where(slot == listed, SLOTS * k + m, place)
+            rank = rank - jnp.where(slot > listed, 1, 0)
+        group = sum(jnp.where(rank >= spare * n, 1, 0) for n in range(1, 4))
+        free = jnp.where(
+            rank < 4 * spare, (SLOTS - spare) * group + MOVE_CAP + rank, 4 * MOVE_CAP + rank
+        )
+        place = jnp.where(place < 0, free, place)
+        position = lax.broadcasted_iota(jnp.int32, (BLOCKS, LANES), 0)
+        held.append(jnp.where(position == place, 1.0, 0.0).astype(BF16))
+        places.append(place)
+
+    def by_position(values, n):
+        rows = jnp.broadcast_to(values.astype(F32), (8, LANES)).astype(BF16)
+        return matmul_t(rows, held[n]).astype(jnp.int32)
+
+    row = lax.broadcasted_iota(jnp.int32, (8, LANES), 0)
+    made = jnp.where(row == ORDER_0, by_position(slot, 0), places[1])
+    made = jnp.where(row == ORDER_1, by_position(slot, 1), made)
+    made = jnp.where(row == SOURCE_1, by_position(places[0], 1), made)
+    tables_made[...] = jnp.clip(made, 0, BLOCKS - 1)
+    tables_copy = pltpu.make_async_copy(tables_made, tables, table_sem)
+    tables_copy.start()
 
     def strided(ref, first, pitch):
         return [ref[pl.ds(first + i, 8, stride=pitch), :] for i in range(FIELDS)]
@@ -410,6 +465,7 @@
     for n, load in enumerate(loads):
         load.wait()
         lax.fori_loop(n * batches // LOADS, (n + 1) * batches // LOADS, scatter_0, 0)
+    tables_copy.wait()
     pl.semaphore_wait(barrier, len(NEAR))
     wait_all(exchange(0))
     velocities(0)
@@ -490,37 +546,12 @@
     lax.fori_loop(0, BLOCKS // 8, put, 0)
 
 
-def slot_tables(move_slots):
-    listed = move_slots.reshape(STEPS, 4 * MOVE_CAP, 1)
-    slot = jnp.arange(BLOCKS, dtype=jnp.int32)
-    same = listed == slot
-    number = jnp.arange(4 * MOVE_CAP, dtype=jnp.int32)[:, None]
-    position = number + (SLOTS - MOVE_CAP) * (number // MOVE_CAP)
-    used = jnp.sum(same.astype(jnp.int32), axis=1)
-    there = jnp.sum(jnp.where(same, position, 0), axis=1)
-    earlier = jnp.sum((listed < slot).astype(jnp.int32), axis=1)
-    rank = slot - earlier
-    spare = 4 * (SLOTS - MOVE_CAP)
-    third = rank // (SLOTS - MOVE_CAP)
-    free = jnp.where(
-        rank < spare,
-        SLOTS * third + MOVE_CAP + rank - (SLOTS - MOVE_CAP) * third,
-        4 * MOVE_CAP + rank,
-    )
-    place = jnp.where(used > 0, there, free)
-    held = place[:, None, :] == slot[None, :, None]
-    order = jnp.sum(jnp.where(held, slot, 0), axis=2)
-    source = jnp.sum(jnp.where(held[1], place[0], 0), axis=1)
-    return jnp.stack([order[0], order[1], source, place[1]])
-
-
 def on_device(particles, anchor_down, anchor_cross, move_count, move_slots):
-    smem = pl.BlockSpec(memory_space=pltpu.SMEM)
     vmem = pl.BlockSpec(memory_space=pltpu.VMEM)
     by_field = pl.pallas_call(
         kernel,
         out_shape=jax.ShapeDtypeStruct((FIELDS, BLOCKS, LANES), F32),
-        in_specs=[smem, smem, smem, smem, pl.BlockSpec(memory_space=pltpu.HBM)],
+        in_specs=[pl.BlockSpec(memory_space=pltpu.HBM)] * 5,
         out_specs=vmem,
         scratch_shapes=[
             pltpu.VMEM((FIELDS, BLOCKS, LANES), F32),
@@ -543,16 +574,29 @@
             pltpu.SemaphoreType.DMA((STEPS, 4)),
             pltpu.SemaphoreType.DMA((STEPS, 4)),
             pltpu.SemaphoreType.DMA((LOADS,)),
+            pltpu.VMEM((8, LANES), jnp.int32),
+            pltpu.SMEM((8, LANES), jnp.int32),
+            pltpu.SemaphoreType.DMA,
+            pltpu.SMEM((STEPS * 4, 1, MOVE_CAP), jnp.int32),
+            pltpu.SMEM((STEPS, BLOCKS), jnp.int32),
+            pltpu.SMEM((STEPS, BLOCKS), jnp.int32),
+            pltpu.SMEM((STEPS, 4), jnp.int32),
+            pltpu.SemaphoreType.DMA((4,)),
         ],
         compiler_params=pltpu.CompilerParams(
             collective_id=0, has_side_effects=True, vmem_limit_bytes=40 * 1024 * 1024
         ),
     )(
-        slot_tables(move_slots),
-        anchor_down,
-        anchor_cross,
-        move_count[:, :, 0, 0],
-        jnp.transpose(particles, (1, 0, 2)),
+        *(
+            pltpu.with_memory_space_constraint(x, pltpu.HBM)
+            for x in (
+                move_slots.reshape(STEPS * 4, 1, MOVE_CAP),
+                anchor_down,
+                anchor_cross,
+                move_count[:, :, 0, 0],
+                jnp.transpose(particles, (1, 0, 2)),
+            )
+        )
     )
     return jnp.transpose(by_field, (1, 0, 2))
 

time: 47.7 us -> 43.6 us (0.914)
  local copies, waits for them, and re-layouts: 3.56 us -> 0.88 us
  other arithmetic: 1.12 us -> 0 us
    unnamed x12 -> x1, local copies, waits for them, and re-layouts: 3.37 us -> 0.88 us
    unnamed x1 -> x0, other arithmetic: 0.67 us -> none
where the time goes in v4:
time: 43.6 us; the launch traced here: 43.5 us
  Pallas kernels  42.6 us (98%)
  local copies, waits for them, and re-layouts  0.88 us (2%)
    pallas_call x1, Pallas kernels, on_device(): pl.pallas_call(kernel, out_shape=jax.ShapeDtypeStruct((FIELDS, BLOCKS, LA...  42.6 us
    unnamed x1, local copies, waits for them, and re-layouts  0.88 us

profile of v4, /device:TPU:6, one launch (start us, length us, event | category | flops | bytes accessed | tf_op | source)
XLA Modules:
  0.0 43.5 jit_solution(17501584348206990564)
XLA Ops:
  0.0 42.6 %shard_map.55 = f32[12,128,128]{2,1,0:T(8,128)S(1)} custom-call(s32[8,1,13]{2,1,0:T(1,128)} %bitcast.8, s32[2,128]{1,0:T(2,128)} %anchor_down_hbm.1, s32[2,128]{1,0:T(2,128)} %anchor_cross_hbm.1, s32[2,4]{1,0:T(2,128)} %bitcast.9, f32[12,128,128]{2,1,0:T(8,128)} %bitcast.7), custom_call_target="tpu_custom_call" | custom-call | tf_op jit(solution)/shard_map/pallas_call | solution.py:551
  42.6 0.9 %copy.8 = f32[128,12,128]{2,0,1:T(8,128)} copy(f32[128,12,128]{2,0,1:T(8,128)S(1)} %bitcast.6) | data formatting | bytes 1572864

commit v5 on v4

--- a/solution.py
+++ b/solution.py
@@ -528,22 +528,25 @@
     lax.fori_loop(2, 4, gather_staying_1, 0)
     wait_all(copies)
 
-    def settle(batch, carry):
-        put_strided(flat_2, batch * 8 * PITCH, PITCH, settled(1, batch))
-        return carry
-
-    lax.fori_loop(0, 8, settle, 0)
-
-    def put(batch, carry):
-        for k in range(8):
-            place = tables[PLACE_1, batch * 8 + k]
+    def settle(group, carry):
+        for n in range(4):
+            batch = 4 * group + n
+            put_strided(flat_2, batch * 8 * PITCH, PITCH, settled(1, batch))
+        return carry
+
+    lax.fori_loop(0, 2, settle, 0)
+
+    def put(group, carry):
+        for k in range(8 * GATHER_BATCHES):
+            place = tables[PLACE_1, group * 8 * GATHER_BATCHES + k]
             stage[PITCH * k : PITCH * k + PITCH, :] = state_2[place]
-        rows = pl.ds(pl.multiple_of(batch * 8, 8), 8)
-        for i, x in enumerate(strided(stage, 0, PITCH)):
-            result[i, rows, :] = x
-        return carry
-
-    lax.fori_loop(0, BLOCKS // 8, put, 0)
+        for n in range(GATHER_BATCHES):
+            rows = pl.ds(pl.multiple_of((group * GATHER_BATCHES + n) * 8, 8), 8)
+            for i, x in enumerate(strided(stage, 8 * PITCH * n, PITCH)):
+                result[i, rows, :] = x
+        return carry
+
+    lax.fori_loop(0, BLOCKS // 8 // GATHER_BATCHES, put, 0)
 
 
 def on_device(particles, anchor_down, anchor_cross, move_count, move_slots):

time: 43.6 us -> 43.4 us (level)
  no operation moved by 1% of the time
where the time goes in v5:
time: 43.4 us; the launch traced here: 43.3 us
  Pallas kernels  42.4 us (98%)
  local copies, waits for them, and re-layouts  0.88 us (2%)
    pallas_call x1, Pallas kernels, on_device(): pl.pallas_call(kernel, out_shape=jax.ShapeDtypeStruct((FIELDS, BLOCKS, LA...  42.4 us
    unnamed x1, local copies, waits for them, and re-layouts  0.88 us

profile of v5, /device:TPU:6, one launch (start us, length us, event | category | flops | bytes accessed | tf_op | source)
XLA Modules:
  0.0 43.3 jit_solution(12250947922845685880)
XLA Ops:
  0.0 42.4 %shard_map.55 = f32[12,128,128]{2,1,0:T(8,128)S(1)} custom-call(s32[8,1,13]{2,1,0:T(1,128)} %bitcast.8, s32[2,128]{1,0:T(2,128)} %anchor_down_hbm.1, s32[2,128]{1,0:T(2,128)} %anchor_cross_hbm.1, s32[2,4]{1,0:T(2,128)} %bitcast.9, f32[12,128,128]{2,1,0:T(8,128)} %bitcast.7), custom_call_target="tpu_custom_call" | custom-call | tf_op jit(solution)/shard_map/pallas_call | solution.py:554
  42.4 0.9 %copy.8 = f32[128,12,128]{2,0,1:T(8,128)} copy(f32[128,12,128]{2,0,1:T(8,128)S(1)} %bitcast.6) | data formatting | bytes 1572864

commit v6 on v5

--- a/solution.py
+++ b/solution.py
@@ -35,7 +35,7 @@
 STRIDE_PAD = 16
 SCATTER_BATCHES = 4
 GATHER_BATCHES = 4
-LOADS = 4
+LOADS = 2
 ORDER_0, ORDER_1, SOURCE_1, PLACE_1 = range(4)
 
 NEAR = ((-1, 0), (1, 0), (0, -1), (0, 1), (-1, -1), (1, -1), (-1, 1), (1, 1))

time: 43.4 us -> 43.4 us (level)
  no operation moved by 1% of the time
where the time goes in v6:
time: 43.4 us; the launch traced here: 43.3 us
  Pallas kernels  42.4 us (98%)
  local copies, waits for them, and re-layouts  0.88 us (2%)
    pallas_call x1, Pallas kernels, on_device(): pl.pallas_call(kernel, out_shape=jax.ShapeDtypeStruct((FIELDS, BLOCKS, LA...  42.4 us
    unnamed x1, local copies, waits for them, and re-layouts  0.88 us

profile of v6, /device:TPU:6, one launch (start us, length us, event | category | flops | bytes accessed | tf_op | source)
XLA Modules:
  0.0 43.3 jit_solution(14247091940843281260)
XLA Ops:
  0.0 42.4 %shard_map.55 = f32[12,128,128]{2,1,0:T(8,128)S(1)} custom-call(s32[8,1,13]{2,1,0:T(1,128)} %bitcast.8, s32[2,128]{1,0:T(2,128)} %anchor_down_hbm.1, s32[2,128]{1,0:T(2,128)} %anchor_cross_hbm.1, s32[2,4]{1,0:T(2,128)} %bitcast.9, f32[12,128,128]{2,1,0:T(8,128)} %bitcast.7), custom_call_target="tpu_custom_call" | custom-call | tf_op jit(solution)/shard_map/pallas_call | solution.py:554
  42.4 0.9 %copy.8 = f32[128,12,128]{2,0,1:T(8,128)} copy(f32[128,12,128]{2,0,1:T(8,128)S(1)} %bitcast.6) | data formatting | bytes 1572864
